TPU v7x, 128 devices: a whole 4x4x4 slice. The times are simulated.
128 devices in a mesh: front: 4 (over y), blk: 32 (over z, x, core).
Axes of the slice: x: 4, y: 4, z: 4, core: 2. Of those that a mesh axis runs over, the one named last changes fastest.
Arguments:
- front_matrix: float32 [4, 13312, 13312], P('front', 'blk')
- random_probe: float32 [4, 13312, 256], P('front', 'blk'), may hold values from -6 to 6
- child_samples: float32 [4, 12288, 256], P('front', 'blk'), may hold values from -6 to 6
- child_dest: int32 [4, 12288], P('front', 'blk'), may hold values from 0 to 13311, as said below
- skeleton: int32 [4, 32, 128], P('front', 'blk'), may hold values from 0 to 415, as said below
- leaf_ranks: int32 [4, 32], P('front', 'blk'), may hold values from 64 to 128, as said below
- pair_skeleton: int32 [4, 16, 128], P('front'), may hold values from 0 to 255, as said below
Outputs:
- interp_leaf: float32 [4, 13312, 128], P('front', 'blk')
- interp_pair: float32 [4, 4096, 128], P('front', 'blk')
Inputs may be any that keep to these rules, and one draw needn't show every extreme that they name: `child_dest`: among the rows of one device, at most 24 name rows of one leaf node; in every group one leaf node of the next group receives exactly 24 rows from every device of the group. `skeleton`: the 128 entries of one leaf are distinct. `leaf_ranks`: 128 is reached in every front. `pair_skeleton`: the 128 entries of one node are distinct and name live slots only: k of leaf 2q with k below its rank, or 128 + k of leaf 2q+1 with k below its rank.
All inputs are finite; a program needn't handle non-finite values.
Results may differ from a plain program's by a relative error of at most 0.0003.
Values sent between devices are 32-bit elements; how exact they have to be, the bound alone decides.
No kernel may reach another device: no remote copies, remote signals or barrier semaphores. Data moves between devices by JAX's collectives and lax.ppermute only.
A program may use at most 192 MiB of HBM per device.

v0:
```python
import jax
import jax.numpy as jnp
from jax import lax
from jax.sharding import Mesh
from jax.sharding import PartitionSpec as P

BLK = ("blk_0", "blk_1", "blk_2")


HIGHEST = lax.Precision.HIGHEST
ridge_share = 0.1


def in_blocks(x, dim, size):
    before, after = (x.shape[:dim], x.shape[dim + 1 :])
    return jnp.moveaxis(x.reshape(*before, size, -1, *after), dim, 0)


def joined_along(parts, dim):
    parts = jnp.moveaxis(parts, 0, dim)
    dims = parts.shape
    return parts.reshape(*dims[:dim], dims[dim] * dims[dim + 1], *dims[dim + 2 :])


def moved_by_axis(parts, axes, sequence):
    dims = [lax.axis_size(a) for a in axes]
    parts = parts.reshape(*dims, *parts.shape[1:])
    for k in sequence:
        parts = lax.all_to_all(parts, axes[k], split_axis=k, concat_axis=k, tiled=True)
    return parts.reshape(-1, *parts.shape[len(axes) :])


def core_and_chips(x, groups, sequence, split_dim, concat_dim):
    size = lax.axis_size(groups[0]) * lax.axis_size(groups[1])
    parts = in_blocks(x, split_dim, size)
    return joined_along(moved_by_axis(parts, groups, sequence), concat_dim)


def from_behind(value, axis, steps):
    count = lax.axis_size(axis)
    pairs = [(source, (source + steps) % count) for source in range(count)]
    return lax.ppermute(value, axis, pairs)


def from_partner(value, axis, stride):
    mask = 2**stride
    pairs = [(source, source ^ mask) for source in range(lax.axis_size(axis))]
    return lax.ppermute(value, axis, pairs)


def exact_dot(left, right):
    return jnp.dot(left, right, precision=HIGHEST, preferred_element_type=jnp.float32)


def interpolate(targets, leaf_basis, live_mask, live_count):
    gram_matrix = exact_dot(leaf_basis, leaf_basis.T)
    ridge_size = ridge_share * jnp.sum(jnp.diagonal(gram_matrix)) / live_count
    gram_matrix = gram_matrix + jnp.diag(jnp.where(live_mask, ridge_size, 1.0))
    factor = jnp.linalg.cholesky(gram_matrix)
    cross_terms = exact_dot(targets, leaf_basis.T)
    return jax.scipy.linalg.cho_solve((factor, True), cross_terms.T).T


def body(
    front_matrix, random_probe, child_samples, child_dest, skeleton, leaf_ranks, pair_skeleton
):
    matrix = front_matrix[0]
    own_probe = random_probe[0]
    height = matrix.shape[0]
    samples = own_probe.shape[1]
    leaf_index = lax.axis_index(BLK)
    pair_index = leaf_index // 2
    lower_half = leaf_index % 2 == 0
    pair_start = pair_index * (2 * height)
    piece_rows = lax.all_gather(own_probe, BLK, axis=0, tiled=True)
    pair_probe = jnp.zeros((2 * height, samples), jnp.float32)
    piece_count = piece_rows.shape[0]
    product = exact_dot(matrix, piece_rows)
    offsets = jnp.arange(piece_count, dtype=jnp.int32) - pair_start
    inside = (offsets >= 0) & (offsets < 2 * height)
    pair_probe = pair_probe.at[jnp.where(inside, offsets, 2 * height)].set(piece_rows, mode="drop")
    product, pair_probe = (product, pair_probe)
    blocks = lax.axis_size(BLK)
    incoming = child_samples[0]
    destinations = child_dest[0]
    count_rows = incoming.shape[0]
    capacity = max(2, (2 * count_rows + blocks - 1) // blocks)
    owner_block = destinations // height
    within = (destinations % height).astype(jnp.float32)
    onehot = (owner_block[:, None] == jnp.arange(blocks, dtype=jnp.int32)[None, :]).astype(
        jnp.int32
    )
    ranking = jnp.sum(jnp.cumsum(onehot, axis=0) * onehot, axis=1) - 1
    places = owner_block * capacity + ranking
    slots_total = blocks * capacity
    sending = jnp.zeros((slots_total, samples), jnp.float32).at[places].set(incoming)
    labels = jnp.full((slots_total,), float(height), jnp.float32).at[places].set(within)
    spread_rows, spread_labels = (
        core_and_chips(sending, (("blk_0", "blk_1"), "blk_2"), (1, 0), 0, 0),
        core_and_chips(labels, (("blk_0", "blk_1"), "blk_2"), (1, 0), 0, 0),
    )
    arrived, arrived_labels = from_behind((spread_rows, spread_labels), "front", 1)
    child_part = jax.ops.segment_sum(
        arrived, arrived_labels.astype(jnp.int32), num_segments=height + 1
    )[:height]
    sample = product + child_part
    diagonal_block = lax.dynamic_slice_in_dim(matrix, leaf_index * height, height, 1)
    off_sample = sample - exact_dot(diagonal_block, own_probe)
    chosen = skeleton[0, 0]
    leaf_rank = leaf_ranks[0, 0]
    live_mask = jnp.arange(chosen.shape[0]) < leaf_rank
    leaf_basis = off_sample[chosen] * live_mask[:, None]
    leaf_interp = interpolate(off_sample, leaf_basis, live_mask, leaf_rank.astype(jnp.float32))
    pair_columns = lax.dynamic_slice_in_dim(matrix, pair_start, 2 * height, 1)[chosen]
    upward = (sample[chosen] - exact_dot(pair_columns, pair_probe)) * live_mask[:, None]
    sibling = from_partner(upward, BLK, 0)
    stacked = jnp.where(
        lower_half, jnp.concatenate([upward, sibling]), jnp.concatenate([sibling, upward])
    )
    pick_rows = lax.dynamic_index_in_dim(pair_skeleton[0], pair_index, 0, keepdims=False)
    pair_basis = stacked[pick_rows]
    pair_width = pick_rows.shape[0]
    pair_interp = interpolate(
        upward, pair_basis, jnp.ones((pair_width,), jnp.bool_), float(pair_width)
    )
    return (leaf_interp[None], pair_interp[None])


def solution(mesh):
    torus = Mesh(
        mesh.devices.reshape(mesh.shape["front"], 4, 4, 2), ("front", "blk_0", "blk_1", "blk_2")
    )
    return jax.shard_map(
        body,
        mesh=torus,
        in_specs=(
            P("front", BLK, None),
            P("front", BLK, None),
            P("front", BLK, None),
            P("front", BLK),
            P("front", BLK, None),
            P("front", BLK),
            P("front", None, None),
        ),
        out_specs=(P("front", BLK, None), P("front", BLK, None)),
        check_vma=False,
    )
```

profile of v0, /device:TPU:1, one launch (start us, length us, event | category | flops | bytes accessed | tf_op | source)
XLA Modules:
  0.0 228.7 jit_solution(11849226646696909378)
XLA Ops:
  7.2 0.7 all-gather.3.cloned.1.call-update
  7.9 0.7 compare_reduce_fusion
  8.6 0.7 fusion.48
  9.4 0.9 reduce-window.6
  10.6 0.7 fusion.40
  11.3 2.1 scatter_custom_fusion.1
  13.4 0.9 copy.36
  14.3 4.9 %all-to-all-start.2 = ((f32[16,2,24,256]{3,2,0,1:T(8,128)}), f32[16,2,24,256]{3,2,0,1:T(8,128)S(1)}, u32[]{:S(2)}, u32[]{:S(2)}) async-start(f32[16,2,24,256]{3,2,0,1:T(8,128)} %copy.36), calls=%async_computation.2 | async-start | bytes 1572864 | tf_op jit(solution)/shard_map/all_to_all | solution.py:29
  19.3 2.9 %scatter_custom_fusion = f32[768]{0:T(1024)S(1)} fusion(s32[384]{0:T(512)S(1)} %fusion.40, f32[384]{0:T(512)S(1)} %get-tuple-element.7, f32[]{:T(128)} %constant.142.clone.1), kind=kCustom, calls=%fused_computation.81 | custom fusion | bytes 3076 | tf_op jit(solution)/shard_map/scatter | solution.py:97
  22.3 0.7 reshape.334
  23.0 3.3 %all-to-all-start = ((f32[2,1,384]{2,1,0:T(1,128)}), f32[2,1,384]{2,1,0:T(1,128)S(1)}, u32[]{:S(2)}, u32[]{:S(2)}) async-start(f32[2,1,384]{2,1,0:T(1,128)} %reshape.334), calls=%async_computation | async-start | bytes 6144 | tf_op jit(solution)/shard_map/all_to_all | solution.py:29
  26.2 1.0 copy.37
  27.2 7.7 %all-to-all-start.3 = ((f32[16,2,24,256]{3,2,1,0:T(8,128)}), f32[16,2,24,256]{3,2,1,0:T(8,128)S(1)}, u32[]{:S(2)}, u32[]{:S(2)}) async-start(f32[16,2,24,256]{3,2,1,0:T(8,128)} %copy.37), calls=%async_computation.3 | async-start | bytes 1572864 | tf_op jit(solution)/shard_map/all_to_all | solution.py:29
  35.6 0.7 reduce.17
  36.4 0.6 copy.35
  37.0 0.7 fusion.46
  37.7 10.8 %all-to-all-done.3 = f32[16,2,24,256]{3,2,1,0:T(8,128)S(1)} async-done(((f32[16,2,24,256]{3,2,1,0:T(8,128)}), f32[16,2,24,256]{3,2,1,0:T(8,128)S(1)}, u32[]{:S(2)}, u32[]{:S(2)}) %all-to-all-start.3) | async-done | bytes 786464 | tf_op jit(solution)/shard_map/all_to_all | solution.py:29
  48.5 3.6 %all-to-all-start.1 = ((f32[16,2,24]{2,1,0:T(2,128)}), f32[16,2,24]{2,1,0:T(2,128)S(1)}, u32[]{:S(2)}, u32[]{:S(2)}) async-start(f32[16,2,24]{2,1,0:T(2,128)} %copy.35), calls=%async_computation.1 | async-start | bytes 32768 | tf_op jit(solution)/shard_map/all_to_all | solution.py:29
  52.2 1.4 collective-permute-start.1
  53.5 0.7 fusion.45
  54.2 2.1 dynamic-slice_bitcast_fusion
  57.0 1.7 all-to-all-done.1
  58.9 1.4 collective-permute-start
  60.2 0.8 gather_fusion.3
  61.1 10.2 %collective-permute-done = f32[768]{0:T(1024)S(1)} collective-permute-done((f32[768]{0:T(1024)S(1)}, f32[768]{0:T(1024)S(1)}, u32[]{:S(2)}, u32[]{:S(2)}) %collective-permute-start) | collective-permute-done | bytes 3104 | tf_op jit(solution)/shard_map/ppermute | solution.py:42
  71.3 6.6 %scatter_custom_fusion.2 = f32[417,256]{1,0:T(8,128)S(1)} fusion(s32[768]{0:T(1024)S(1)} %convert_element_type.25, f32[768,256]{1,0:T(8,128)} %collective-permute-done.1, f32[]{:T(128)} %constant.141.clone.1), kind=kCustom, calls=%fused_computation.29 | custom fusion | flops 196608 | bytes 427520 | tf_op jit(solution)/shard_map/scatter-add | solution.py:103
  78.0 3.8 %all-gather.3.cloned.1.call-done = f32[1,13312,256]{2,1,0:T(8,128)} async-done(((f32[1,416,256]{2,1,0:T(8,128)}), f32[1,13312,256]{2,1,0:T(8,128)}) %all-gather.3.cloned.1.call-update) | async-done | bytes 13631504 | tf_op jit(solution)/shard_map/all_gather | solution.py:75
  81.8 21.9 %slice_add_fusion = f32[416,256]{1,0:T(8,128)S(1)} fusion(f32[417,256]{1,0:T(8,128)S(1)} %scatter_custom_fusion.2, f32[1,13312,256]{2,1,0:T(8,128)} %all-gather.3.cloned.1.call-done, f32[1,416,13312]{2,1,0:T(8,128)} %param.8), kind=kOutput, calls=%fused_computation.21 | convolution fusion | flops 17012203520 | bytes 36634624 | tf_op jit(solution)/shard_map/dot_general | solution.py:52
  103.6 0.8 gather_fusion.2
  104.4 2.2 convolution_subtract_fusion
  106.6 0.8 gather_fusion
  108.3 1.5 gather_fusion.1
  109.8 0.6 reduce_sum.28
  111.5 11.7 %cholesky.44 = f32[128,128]{1,0:T(8,128)S(1)} custom-call(f32[128,128]{1,0:T(8,128)S(1)} %copy.39), custom_call_target="Cholesky" | custom-call | tf_op jit(solution)/shard_map/jit(cholesky)/cholesky | solution.py:59
  123.2 0.6 compare_reduce_fusion.2
  123.9 0.7 fusion.18
  124.5 9.8 %custom-call.16 = f32[1,128,128]{1,2,0:T(8,128)S(1)} custom-call(f32[1,128,128]{2,1,0:T(8,128)S(1)} %fusion.18), custom_call_target="InvertDiagBlocksLowerTriangular" | custom-call | tf_op jit(solution)/shard_map/jit(_cho_solve)/triangular_solve | solution.py:61
  134.4 56.6 %scatter_custom_fusion.3 = f32[832,256]{1,0:T(8,128)S(1)} fusion(s32[13312]{0:T(1024)S(1)} %bitcast.124, f32[1,13312,256]{2,1,0:T(8,128)} %all-gather.3.cloned.1.call-done, f32[]{:T(128)} %constant.141.clone.1), kind=kCustom, calls=%fused_computation.12 | custom fusion | bytes 14483460 | tf_op jit(solution)/shard_map/scatter | solution.py:81
  191.0 0.6 fusion.49
  192.3 1.0 convolution_bitcast_fusion
  193.4 0.8 gather_fusion.4
  194.7 1.5 gather_fusion.5
  196.2 0.6 reduce_sum.29
  197.7 11.7 %cholesky.55 = f32[128,128]{1,0:T(8,128)S(1)} custom-call(f32[128,128]{1,0:T(8,128)S(1)} %copy.41), custom_call_target="Cholesky" | custom-call | tf_op jit(solution)/shard_map/jit(cholesky)/cholesky | solution.py:59
  209.5 0.6 compare_reduce_fusion.1
  210.1 0.7 fusion.19
  210.8 9.8 %custom-call.17 = f32[1,128,128]{1,2,0:T(8,128)S(1)} custom-call(f32[1,128,128]{2,1,0:T(8,128)S(1)} %fusion.19), custom_call_target="InvertDiagBlocksLowerTriangular" | custom-call | tf_op jit(solution)/shard_map/jit(_cho_solve)/triangular_solve | solution.py:61
  220.9 0.9 convolution_bitcast_fusion.1
  (47 shorter events, 4.6 us)
Async XLA Ops:
  7.2 4.2 %copy-start = (f32[1,384,256]{2,1,0:T(8,128)S(1)}, f32[1,384,256]{2,1,0:T(8,128)}, u32[]{:S(2)}) copy-start(f32[1,384,256]{2,1,0:T(8,128)} %param.10) | copy-start | bytes 1179652
  7.2 74.6 %all-gather.3.cloned.1.call-start = ((), (), s32[]{:S(2)}) async-start(), calls=%async_computation.4 | async-start | bytes 14057472 | tf_op jit(solution)/shard_map/all_gather | solution.py:75
  14.3 8.6 %all-to-all-start.2 = ((f32[16,2,24,256]{3,2,0,1:T(8,128)}), f32[16,2,24,256]{3,2,0,1:T(8,128)S(1)}, u32[]{:S(2)}, u32[]{:S(2)}) async-start(f32[16,2,24,256]{3,2,0,1:T(8,128)} %copy.36), calls=%async_computation.2 | async-start | bytes 1572864 | tf_op jit(solution)/shard_map/all_to_all | solution.py:29
  23.0 4.3 %all-to-all-start = ((f32[2,1,384]{2,1,0:T(1,128)}), f32[2,1,384]{2,1,0:T(1,128)S(1)}, u32[]{:S(2)}, u32[]{:S(2)}) async-start(f32[2,1,384]{2,1,0:T(1,128)} %reshape.334), calls=%async_computation | async-start | bytes 6144 | tf_op jit(solution)/shard_map/all_to_all | solution.py:29
  27.2 21.3 %all-to-all-start.3 = ((f32[16,2,24,256]{3,2,1,0:T(8,128)}), f32[16,2,24,256]{3,2,1,0:T(8,128)S(1)}, u32[]{:S(2)}, u32[]{:S(2)}) async-start(f32[16,2,24,256]{3,2,1,0:T(8,128)} %copy.37), calls=%async_computation.3 | async-start | bytes 1572864 | tf_op jit(solution)/shard_map/all_to_all | solution.py:29
  48.5 10.2 %all-to-all-start.1 = ((f32[16,2,24]{2,1,0:T(2,128)}), f32[16,2,24]{2,1,0:T(2,128)S(1)}, u32[]{:S(2)}, u32[]{:S(2)}) async-start(f32[16,2,24]{2,1,0:T(2,128)} %copy.35), calls=%async_computation.1 | async-start | bytes 32768 | tf_op jit(solution)/shard_map/all_to_all | solution.py:29
  52.2 19.1 %collective-permute-start.1 = (f32[768,256]{1,0:T(8,128)S(1)}, f32[768,256]{1,0:T(8,128)}, u32[]{:S(2)}, u32[]{:S(2)}) collective-permute-start(f32[768,256]{1,0:T(8,128)S(1)} %bitcast.121), channel_id=1, source_target_pairs={{0,32},{32,64},{64,96},{96,0},{1,33},{33,65},{65,97},{97,1},{2,34}... | collective-permute-start | bytes 2359304 | tf_op jit(solution)/shard_map/ppermute | solution.py:42
  58.9 12.4 %collective-permute-start = (f32[768]{0:T(1024)S(1)}, f32[768]{0:T(1024)S(1)}, u32[]{:S(2)}, u32[]{:S(2)}) collective-permute-start(f32[768]{0:T(1024)S(1)} %reshape_reshape.13), channel_id=1, source_target_pairs={{0,32},{32,64},{64,96},{96,0},{1,33},{33,65},{65,97},{97,1},{2,34}... | collective-permute-start | bytes 9224 | tf_op jit(solution)/shard_map/ppermute | solution.py:42
  77.9 26.4 %copy-start.1 = (f32[1,416,256]{2,1,0:T(8,128)S(1)}, f32[1,416,256]{2,1,0:T(8,128)}, u32[]{:S(2)}) copy-start(f32[1,416,256]{2,1,0:T(8,128)} %param.9) | copy-start | bytes 1277956
  191.7 1.7 collective-permute-start.2
Sparse Core Ops, SparseCore 0:
  10.2 71.4 all-gather.2
where the time goes:
time: 229 us
  local copies, waits for them, and re-layouts  74.3 us (32%)
  other arithmetic  59.2 us (26%)
  matrix products  28.7 us (13%)
  waiting for transfers between devices  27.4 us (12%)
  starting transfers between devices  22.6 us (10%)
  between operations  16.4 us (7%)
    scatter x1, local copies, waits for them, and re-layouts, body(): pair_probe.at[jnp.where(inside, offsets, 2 * height)]  56.6 us
    dot_general x7, matrix products, exact_dot(): jnp.dot(left, right, precision=HIGHEST, preferred_element_type=jnp.float32)  26.2 us
    another operation x6, other arithmetic, interpolate(): factor = jnp.linalg.cholesky(gram_matrix)  24.8 us
    another operation x4, other arithmetic, interpolate(): return jax.scipy.linalg.cho_solve((factor, True), cross_terms.T).T  20.9 us
    all_to_all x4, starting transfers between devices, moved_by_axis(): lax.all_to_all(parts, axes[k], split_axis=k, concat_axis=k, tiled=True)  19.5 us
    all_to_all x4, waiting for transfers between devices, moved_by_axis(): lax.all_to_all(parts, axes[k], split_axis=k, concat_axis=k, tiled=True)  12.6 us
    ppermute x2, waiting for transfers between devices, from_behind(): return lax.ppermute(value, axis, pairs)  10.2 us
    scatter-add x1, other arithmetic, body(): jax.ops.segment_sum(arrived, arrived_labels.astype(jnp.int32), num_segmen...  6.63 us
  transfers between devices with their start and end apart: 8, of which 4 were waited for; matrix products, arithmetic and copies ran while one was open for 11% of the time, Pallas kernels for 0%

commit v1 on v0

v1 whole, which is shorter than its diff:
```python
import jax
import jax.numpy as jnp
from jax import lax
from jax.experimental import pallas as pl
from jax.experimental.pallas import tpu as pltpu
from jax.sharding import Mesh
from jax.sharding import PartitionSpec as P


BLK = ("blk_0", "blk_1", "blk_2")

f32, bf16 = jnp.float32, jnp.bfloat16
HIGHEST = lax.Precision.HIGHEST
ridge_share = 0.1
HEIGHT, SAMPLES, RANK = 416, 256, 128
CAP, WIDE, GROUP = 24, 512, 56

TREE = (
    ((1, 0), (0, 0), "p", 1),
    ((3, 0), (0, 0), "p", -1),
    ((0, 1), (0, 0), "q", 1),
    ((0, 3), (0, 0), "q", -1),
    ((2, 0), (1, 0), "p", 1),
    ((1, 3), (1, 0), "q", -1),
    ((3, 1), (3, 0), "q", 1),
    ((1, 1), (1, 0), "q", 1),
    ((3, 3), (3, 0), "q", -1),
    ((3, 2), (3, 1), "q", 1),
    ((1, 2), (1, 3), "q", -1),
    ((0, 2), (0, 1), "q", 1),
    ((2, 3), (2, 0), "q", -1),
    ((2, 2), (3, 2), "p", -1),
    ((2, 1), (2, 0), "q", 1),
)
GROUPS = (
    ((1, 0), (3, 0)),
    ((0, 1), (0, 3), (2, 0)),
    ((1, 3), (3, 1), (1, 1)),
    ((3, 3), (3, 2), (1, 2)),
    ((0, 2), (2, 3)),
    ((2, 2), (2, 1)),
)


def chips_step(value, kind, step):
    def at(z, x, c):
        return ((z % 4) * 4 + x % 4) * 2 + c

    pairs = []
    for z in range(4):
        for x in range(4):
            for c in range(2):
                along_x = (kind == "p") == (c == 0)
                pairs.append((at(z, x, c), at(z, x + step, c) if along_x else at(z + step, x, c)))
    return lax.ppermute(value, BLK, pairs)


def swap_cores(value):
    return lax.ppermute(value, "blk_2", [(0, 1), (1, 0)])


def split2(x):
    hi = x.astype(bf16)
    return hi, (x - hi.astype(f32)).astype(bf16)


def split3(x):
    hi = x.astype(bf16)
    rest = x - hi.astype(f32)
    mid = rest.astype(bf16)
    return hi, mid, (rest - mid.astype(f32)).astype(bf16)


def mxu(a, b, dims):
    return lax.dot_general(a, b, (dims, ((), ())), preferred_element_type=f32)


NN, NT, TN = ((1,), (0,)), ((1,), (1,)), ((0,), (0,))


def dot3(a, b, dims):
    ah, al = split2(a)
    bh, bl = split2(b)
    return mxu(al, bh, dims) + mxu(ah, bl, dims) + mxu(ah, bh, dims)


def pack_kernel(rows_ref, dest_ref, out_ref):
    count = rows_ref.shape[0]
    dest = dest_ref[...].astype(f32)
    leaf_id = lax.broadcasted_iota(jnp.int32, (32, count), 0).astype(f32)
    low = leaf_id * float(HEIGHT)
    member = ((dest >= low) & (dest < low + float(HEIGHT))).astype(f32)
    earlier = lax.broadcasted_iota(jnp.int32, (count, count), 0) < lax.broadcasted_iota(
        jnp.int32, (count, count), 1
    )
    before = mxu(member.astype(bf16), earlier.astype(f32).astype(bf16), NN)
    place = jnp.sum(member * before, axis=0, keepdims=True)
    leaf = jnp.sum(member * leaf_id, axis=0, keepdims=True)
    chip = jnp.floor(leaf * 0.5)
    within = dest - leaf * float(HEIGHT)
    slot = (leaf - 2.0 * chip) * float(CAP) + place
    where = (chip * float(GROUP) + slot).astype(jnp.int32)
    total = 16 * GROUP
    chosen = lax.broadcasted_iota(jnp.int32, (total, count), 0) == where
    chosen = chosen.astype(f32).astype(bf16)
    hi, lo = split2(rows_ref[...])
    out_ref[...] = mxu(chosen, hi, NN) + mxu(chosen, lo, NN)
    chip_id = lax.broadcasted_iota(jnp.int32, (16, count), 0).astype(f32)
    lane_id = lax.broadcasted_iota(jnp.int32, (128, count), 0).astype(f32)
    labels = lax.dot_general(
        jnp.where(chip == chip_id, within, 0.0),
        (slot == lane_id).astype(f32),
        (NT, ((), ())),
        precision=HIGHEST,
        preferred_element_type=f32,
    )
    for j in range(16):
        out_ref[j * GROUP + 2 * CAP : j * GROUP + 2 * CAP + 1, 0:128] = labels[j : j + 1, :]


def pack(rows, dest):
    return pl.pallas_call(
        pack_kernel,
        out_shape=jax.ShapeDtypeStruct((16 * GROUP, SAMPLES), f32),
        compiler_params=pltpu.CompilerParams(vmem_limit_bytes=24 * 1024 * 1024),
        cost_estimate=pl.CostEstimate(flops=400_000_000, bytes_accessed=2_000_000, transcendentals=0),
    )(rows, dest)


def unpack_kernel(where_ref, in_ref, mine_ref, other_ref, label_ref):
    label_ref[...] = jnp.zeros_like(label_ref)
    for j in range(16):
        label_ref[j : j + 1, :] = in_ref[j, 2 * CAP : 2 * CAP + 1, 0:128]
    labels = label_ref[...].T
    row_id = lax.broadcasted_iota(jnp.int32, (CAP, HEIGHT), 1).astype(f32)
    sums = []
    for half in range(2):
        lo_row = half * CAP
        picks = jnp.concatenate(
            [(labels[lo_row : lo_row + CAP, j : j + 1] == row_id).astype(f32) for j in range(16)],
            axis=0,
        ).astype(bf16)
        rows = in_ref[:, lo_row : lo_row + CAP, :].reshape(16 * CAP, SAMPLES)
        hi, lo = split2(rows)
        sums.append(mxu(picks, hi, TN) + mxu(picks, lo, TN))
    first = where_ref[2] == 0
    mine_ref[...] = jnp.where(first, sums[0], sums[1])
    other_ref[...] = jnp.where(first, sums[1], sums[0])


def unpack(where, arrived):
    half = jax.ShapeDtypeStruct((HEIGHT, SAMPLES), f32)
    vmem = pl.BlockSpec(memory_space=pltpu.VMEM)
    return pl.pallas_call(
        unpack_kernel,
        out_shape=(half, half),
        in_specs=[pl.BlockSpec(memory_space=pltpu.SMEM), vmem],
        out_specs=(vmem, vmem),
        scratch_shapes=[pltpu.VMEM((128, 128), f32)],
        compiler_params=pltpu.CompilerParams(vmem_limit_bytes=24 * 1024 * 1024),
        cost_estimate=pl.CostEstimate(flops=400_000_000, bytes_accessed=2_000_000, transcendentals=0),
    )(where, arrived)


def leaf_of(where_ref, block, sibling):
    z, x, c = where_ref[0], where_ref[1], where_ref[2]
    p, q = block
    if sibling:
        c = 1 - c
    first = c == 0
    from_z = lax.rem(z + 4 - jnp.where(first, q, p), 4)
    from_x = lax.rem(x + 4 - jnp.where(first, p, q), 4)
    return (from_z * 4 + from_x) * 2 + c


def product_kernel(blocks, first, last, *refs):
    refs = list(refs)
    where_ref, rank_ref, matrix_ref = refs[:3]
    refs = refs[3:]
    probes, refs = refs[: len(blocks)], refs[len(blocks) :]
    if first:
        out_ref, near_ref, wide, high, low, sem = refs
    elif last:
        total_ref, mine_ref, other_ref, chosen_ref, out_ref, up_ref, wide, high, low, sem = refs
    else:
        total_ref, out_ref, wide, high, low, sem = refs
    leaves = [leaf_of(where_ref, *b) for b in blocks]
    copies = []
    for k, leaf in enumerate(leaves):
        start = pl.multiple_of((leaf * 13) // 4 * 128, 128)
        copies.append(
            pltpu.make_async_copy(matrix_ref.at[:, pl.ds(start, WIDE)], wide.at[k], sem.at[k])
        )
        copies[-1].start()
    total = None if first else total_ref[...]
    for k, leaf in enumerate(leaves):
        slot = k % 2
        for hold in (high, low):
            hold[slot, 0:96, :] = jnp.zeros((96, SAMPLES), bf16)
            hold[slot, HEIGHT:WIDE, :] = jnp.zeros((96, SAMPLES), bf16)
        copies[k].wait()
        offset = pl.multiple_of(lax.rem(leaf, 4) * 32, 32)
        hi, lo = split2(probes[k][...])
        high[slot, pl.ds(offset, HEIGHT), :] = hi
        low[slot, pl.ds(offset, HEIGHT), :] = lo
        xh, xl = high[slot], low[slot]
        parts = []
        for rows in (slice(0, 208), slice(208, 416)):
            mh, ml = split2(wide[k, rows, :])
            left = jnp.concatenate([ml, mh, mh], axis=1)
            right = jnp.concatenate([xh, xl, xh], axis=0)
            parts.append(mxu(left, right, NN))
        term = jnp.concatenate(parts, axis=0)
        if first and k == 0:
            near_ref[...] = term
        else:
            total = term if total is None else total + term
    if last:
        total = total + (mine_ref[...] + other_ref[...])
        picks = pick_matrix(chosen_ref[...], HEIGHT)
        live = lax.broadcasted_iota(jnp.int32, (RANK, SAMPLES), 0) < rank_ref[0]
        up_ref[...] = jnp.where(live, take(picks, total), 0.0)
    out_ref[...] = total


def pick_matrix(row, width):
    column = jnp.broadcast_to(row.astype(f32), (RANK, RANK)).T
    parts = []
    for start in range(0, width, RANK):
        size = min(RANK, width - start)
        lane = lax.broadcasted_iota(jnp.int32, (RANK, size), 1).astype(f32) + float(start)
        parts.append((column[:, :size] == lane).astype(f32))
    return jnp.concatenate(parts, axis=1).astype(bf16)


def take(picks, values):
    hi, mid, lo = split3(values)
    return (mxu(picks, lo, NN) + mxu(picks, mid, NN)) + mxu(picks, hi, NN)


def product(where, rank, matrix, blocks, probes, total=None, last=None):
    count = len(blocks)
    smem = pl.BlockSpec(memory_space=pltpu.SMEM)
    vmem = pl.BlockSpec(memory_space=pltpu.VMEM)
    args = [where, rank, matrix, *probes]
    specs = [smem, smem, pl.BlockSpec(memory_space=pltpu.HBM)] + [vmem] * count
    out_shape = [jax.ShapeDtypeStruct((HEIGHT, SAMPLES), f32)]
    first = total is None
    if first:
        out_shape.append(jax.ShapeDtypeStruct((HEIGHT, SAMPLES), f32))
    else:
        args.append(total)
        specs.append(vmem)
    if last is not None:
        args += list(last)
        specs += [vmem] * len(last)
        out_shape.append(jax.ShapeDtypeStruct((RANK, SAMPLES), f32))

    def kernel(*refs):
        product_kernel(blocks, first, last is not None, *refs)

    out = pl.pallas_call(
        kernel,
        out_shape=tuple(out_shape),
        in_specs=specs,
        out_specs=tuple([vmem] * len(out_shape)),
        scratch_shapes=[
            pltpu.VMEM((count, HEIGHT, WIDE), f32),
            pltpu.VMEM((2, WIDE, SAMPLES), bf16),
            pltpu.VMEM((2, WIDE, SAMPLES), bf16),
            pltpu.SemaphoreType.DMA((count,)),
        ],
        compiler_params=pltpu.CompilerParams(vmem_limit_bytes=44 * 1024 * 1024),
        cost_estimate=pl.CostEstimate(
            flops=count * 6 * HEIGHT * WIDE * SAMPLES,
            bytes_accessed=count * 4 * HEIGHT * (WIDE + SAMPLES),
            transcendentals=0,
        ),
    )(*args)
    return out if len(out_shape) > 1 else out[0]


def total_of(terms):
    while len(terms) > 1:
        terms = [sum(terms[i + 1 : i + 2], terms[i]) for i in range(0, len(terms), 2)]
    return terms[0]


def small_inverse(s):
    n = len(s)
    if n == 2:
        r = 1.0 / (s[0][0] * s[1][1] - s[0][1] * s[0][1])
        off = -(s[0][1] * r)
        return [[s[1][1] * r, off], [off, s[0][0] * r]]
    h = n // 2
    span = range(h)
    b = [[s[i][h + j] for j in span] for i in span]
    p = small_inverse([[s[i][j] for j in span] for i in span])
    w = [[total_of([p[i][k] * b[k][j] for k in span]) for j in span] for i in span]
    rest = [[None] * h for _ in span]
    for i in span:
        for j in range(i, h):
            rest[i][j] = rest[j][i] = s[h + i][h + j] - total_of([b[k][i] * w[k][j] for k in span])
    q = small_inverse(rest)
    e = [[total_of([w[i][k] * q[k][j] for k in span]) for j in span] for i in span]
    out = [[None] * n for _ in range(n)]
    for i in span:
        for j in span:
            out[i][h + j] = out[h + j][i] = -e[i][j]
            out[h + i][h + j] = q[i][j]
            if j >= i:
                out[i][j] = out[j][i] = p[i][j] + total_of([e[i][k] * w[j][k] for k in span])
    return out


def by_position(index, values):
    bit = 1
    while len(values) > 1:
        odd = (index & bit) != 0
        values = [jnp.where(odd, values[i + 1], values[i]) for i in range(0, len(values), 2)]
        bit *= 2
    return values[0]


def eliminate(panel, at, first):
    lane = lax.broadcasted_iota(jnp.int32, (8, RANK), 1)
    sub = lax.broadcasted_iota(jnp.int32, (8, RANK), 0)
    inside = (lane >= first) & (lane < first + 8)
    tile = panel[at]
    rows = [jnp.broadcast_to(tile[a : a + 1, :], (8, RANK)) for a in range(8)]
    s = [[None] * 8 for _ in range(8)]
    for a in range(8):
        for b in range(a, 8):
            s[a][b] = s[b][a] = jnp.broadcast_to(rows[a][:, first + b : first + b + 1], (8, RANK))
    d = small_inverse(s)
    scaled = []
    for a in range(8):
        own = by_position(lane, d[a])
        scaled.append(jnp.where(inside, own, total_of([d[a][b] * rows[b] for b in range(8)])))
    out = []
    for t, old in enumerate(panel):
        if t == at:
            out.append(by_position(sub, scaled))
            continue
        columns = [jnp.broadcast_to(old[:, first + a : first + a + 1], (8, RANK)) for a in range(8)]
        out.append(jnp.where(inside, 0.0, old) - total_of([c * r for c, r in zip(columns, scaled)]))
    return out


def invert(refs, tiles=8):
    lane = lax.broadcasted_iota(jnp.int32, (RANK, RANK), 1)
    row = lax.broadcasted_iota(jnp.int32, (RANK, RANK), 0)
    height = 8 * tiles
    for start in range(0, RANK, height):
        panels = [[ref[start + 8 * t : start + 8 * t + 8, :] for t in range(tiles)] for ref in refs]
        for t in range(tiles):
            panels = [eliminate(panel, t, start + 8 * t) for panel in panels]
        for ref, panel in zip(refs, panels):
            old = ref[...]
            inside = (lane >= start) & (lane < start + height)
            new = jnp.concatenate(panel, axis=0)
            zeros = lambda n: [jnp.zeros((n, RANK), f32)] if n else []
            full = jnp.concatenate(zeros(start) + [new] + zeros(RANK - start - height), axis=0)
            ch, cm, cl = split3(jnp.where(inside, old, 0.0))
            rh, rm, rl = split3(full)
            change = mxu(
                jnp.concatenate([cl, cm, ch, cm, ch, ch], axis=1),
                jnp.concatenate([rh, rm, rl, rh, rm, rh], axis=0),
                NN,
            )
            in_panel = (row >= start) & (row < start + height)
            ref[...] = jnp.where(in_panel, full, jnp.where(inside, 0.0, old) - change)


def system_of(basis, live, count):
    gram = dot3(basis, basis, NT)
    ridge = ridge_share * jnp.sum(basis * basis, keepdims=True) / count
    i = lax.broadcasted_iota(jnp.int32, (RANK, RANK), 0)
    j = lax.broadcasted_iota(jnp.int32, (RANK, RANK), 1)
    shift = jnp.broadcast_to(ridge, (RANK, RANK))
    if live is not None:
        shift = jnp.where(i < live, shift, 1.0)
    return gram + jnp.where(i == j, shift, 0.0)


def finish_kernel(
    where_ref, rank_ref, sum_ref, near_ref, up_ref, sibling_ref, chosen_ref, pick_ref, leaf_ref, pair_ref, hold
):
    rank = rank_ref[0]
    off = sum_ref[...] + near_ref[...]
    live = lax.broadcasted_iota(jnp.int32, (RANK, SAMPLES), 0) < rank
    basis = jnp.where(live, take(pick_matrix(chosen_ref[...], HEIGHT), off), 0.0)
    up = up_ref[...]
    pick = pick_ref[...]
    pick = jnp.where(where_ref[2] == 0, pick, (pick + RANK) & (2 * RANK - 1))
    picks = pick_matrix(pick, 2 * RANK)
    pair_basis = take(picks[:, :RANK], up) + take(picks[:, RANK:], sibling_ref[...])
    hold[0] = system_of(basis, rank, rank.astype(f32))
    hold[1] = system_of(pair_basis, None, float(RANK))
    leaf_cross = dot3(off, basis, NT)
    pair_cross = dot3(up, pair_basis, NT)
    invert([hold.at[0], hold.at[1]])
    leaf_ref[...] = dot3(leaf_cross, hold[0], NN)
    pair_ref[...] = dot3(pair_cross, hold[1], NN)


def finish(where, rank, total, near, upward, sibling, chosen, pick):
    smem = pl.BlockSpec(memory_space=pltpu.SMEM)
    vmem = pl.BlockSpec(memory_space=pltpu.VMEM)
    return pl.pallas_call(
        finish_kernel,
        out_shape=(
            jax.ShapeDtypeStruct((HEIGHT, RANK), f32),
            jax.ShapeDtypeStruct((RANK, RANK), f32),
        ),
        in_specs=[smem, smem] + [vmem] * 6,
        out_specs=(vmem, vmem),
        scratch_shapes=[pltpu.VMEM((2, RANK, RANK), f32)],
        compiler_params=pltpu.CompilerParams(vmem_limit_bytes=24 * 1024 * 1024),
        cost_estimate=pl.CostEstimate(flops=2_000_000_000, bytes_accessed=2_000_000, transcendentals=0),
    )(where, rank, total, near, upward, sibling, chosen, pick)


def body(
    front_matrix, random_probe, child_samples, child_dest, skeleton, leaf_ranks, pair_skeleton
):
    matrix, own = front_matrix[0], random_probe[0]
    z, x, c = lax.axis_index("blk_0"), lax.axis_index("blk_1"), lax.axis_index("blk_2")
    where = jnp.stack([z, x, c]).astype(jnp.int32)
    rank = leaf_ranks[0]
    chosen = skeleton[0]
    pick = lax.dynamic_slice_in_dim(pair_skeleton[0], z * 4 + x, 1, 0)

    ahead = [(k, (k + 1) % 4) for k in range(4)]
    got = {(0, 0): own}
    for arrives, sent, kind, step in TREE:
        got[arrives] = chips_step(got[sent], kind, step)
    rows = lax.ppermute(child_samples[0], "front", ahead)
    dest = lax.ppermute(child_dest, "front", ahead)
    sending = pack(rows, dest).reshape(16, GROUP, SAMPLES)
    arrived = lax.all_to_all(sending, ("blk_0", "blk_1"), 0, 0, tiled=True)
    mine, other = unpack(where, arrived)
    other = swap_cores(other)
    near_probe = swap_cores(own)
    total = near = None
    for n, group in enumerate(GROUPS):
        blocks = [(b, s) for s in (False, True) for b in group]
        probes = [got[b] for b in group] + [swap_cores(got[b]) for b in group]
        if n == 0:
            blocks, probes = [((0, 0), True)] + blocks, [near_probe] + probes
        last = (mine, other, chosen) if n == len(GROUPS) - 1 else None
        total = product(where, rank, matrix, blocks, probes, total, last)
        if n == 0:
            total, near = total
    total, upward = total
    sibling = swap_cores(upward)
    leaf_interp, pair_interp = finish(where, rank, total, near, upward, sibling, chosen, pick)
    return (leaf_interp[None], pair_interp[None])


def solution(mesh):
    torus = Mesh(
        mesh.devices.reshape(mesh.shape["front"], 4, 4, 2), ("front", "blk_0", "blk_1", "blk_2")
    )
    return jax.shard_map(
        body,
        mesh=torus,
        in_specs=(
            P("front", BLK, None),
            P("front", BLK, None),
            P("front", BLK, None),
            P("front", BLK),
            P("front", BLK, None),
            P("front", BLK),
            P("front", None, None),
        ),
        out_specs=(P("front", BLK, None), P("front", BLK, None)),
        check_vma=False,
    )
```

time: 229 us -> 125 us (0.55)
  local copies, waits for them, and re-layouts: 74.3 us -> 15.1 us
  other arithmetic: 59.2 us -> 0.08 us
  Pallas kernels: 0 us -> 41.6 us
  matrix products: 28.7 us -> 0 us
  starting transfers between devices: 22.6 us -> 40.4 us
  between operations: 16.4 us -> 1.53 us
    scatter x3 -> x0, local copies, waits for them, and re-layouts: 61.6 us -> none  [the longest x1 56.6 us: body(): pair_probe.at[jnp.where(inside, offsets, 2 * height)]]
    another operation x12 -> x1, other arithmetic: 46.6 us -> 0.08 us  [body(): where = jnp.stack([z, x, c]).astype(jnp.int32)]
    pallas_call x0 -> x9, Pallas kernels: none -> 41.6 us  [the longest x6 29.7 us: product(): pl.pallas_call(kernel, out_shape=tuple(out_shape), in_specs=specs, out_sp...]
    ppermute x3 -> x35, starting transfers between devices: 3.06 us -> 36.3 us  [the longest x15 18.6 us: chips_step(): return lax.ppermute(value, BLK, pairs)]
    dot_general x7 -> x0, matrix products: 26.2 us -> none  [exact_dot(): jnp.dot(left, right, precision=HIGHEST, preferred_element_type=jnp.float32)]
    ppermute x3 -> x35, waiting for transfers between devices: 10.2 us -> 26.1 us  [the longest x15 15.9 us: chips_step(): return lax.ppermute(value, BLK, pairs)]
    all_to_all x4 -> x1, starting transfers between devices: 19.5 us -> 4.12 us  [body(): arrived = lax.all_to_all(sending, ('blk_0', 'blk_1'), 0, 0, tiled=True)]
    unnamed x6 -> x40, local copies, waits for them, and re-layouts: 0.77 us -> 15.1 us
  transfers between devices with their start and end apart: 8 -> 36, of which waited for: 4 -> 6; matrix products, arithmetic and copies ran while one was open for 11% -> 0% of each run, Pallas kernels for 0% -> 23%
where the time goes in v1:
time: 125 us
  Pallas kernels  41.6 us (33%)
  starting transfers between devices  40.4 us (32%)
  waiting for transfers between devices  26.1 us (21%)
  local copies, waits for them, and re-layouts  15.1 us (12%)
  between operations  1.53 us (1%)
    pallas_call x6, Pallas kernels, product(): pl.pallas_call(kernel, out_shape=tuple(out_shape), in_specs=specs, out_sp...  29.7 us
    ppermute x15, starting transfers between devices, chips_step(): return lax.ppermute(value, BLK, pairs)  18.6 us
    ppermute x15, waiting for transfers between devices, chips_step(): return lax.ppermute(value, BLK, pairs)  15.9 us
    ppermute x18, starting transfers between devices, swap_cores(): return lax.ppermute(value, 'blk_2', [(0, 1), (1, 0)])  15.2 us
    unnamed x40, local copies, waits for them, and re-layouts  15.1 us
    ppermute x1, waiting for transfers between devices, body(): dest = lax.ppermute(child_dest, 'front', ahead)  9.06 us
    pallas_call x1, Pallas kernels, finish(): pl.pallas_call(finish_kernel, out_shape=(jax.ShapeDtypeStruct((HEIGHT, RA...  8.39 us
    all_to_all x1, starting transfers between devices, body(): arrived = lax.all_to_all(sending, ('blk_0', 'blk_1'), 0, 0, tiled=True)  4.12 us
  transfers between devices with their start and end apart: 36, of which 6 were waited for; matrix products, arithmetic and copies ran while one was open for 0% of the time, Pallas kernels for 23%

profile of v1, /device:TPU:1, one launch (start us, length us, event | category | flops | bytes accessed | tf_op | source)
XLA Modules:
  0.0 124.8 jit_solution(47228052022152032)
XLA Ops:
  0.6 2.5 %collective-permute-start.4 = (f32[416,256]{1,0:T(8,128)}, f32[416,256]{1,0:T(8,128)S(1)}, u32[]{:S(2)}, u32[]{:S(2)}) collective-permute-start(f32[416,256]{1,0:T(8,128)} %bitcast.28), channel_id=1, source_target_pairs={{0,2},{1,9},{2,4},{3,11},{4,6},{5,13},{6,0},{7,15},{8,10},{9,17},{... | collective-permute-start | bytes 1277960 | tf_op jit(solution)/shard_map/ppermute | solution.py:55
  3.2 2.2 %collective-permute-start = (f32[416,256]{1,0:T(8,128)}, f32[416,256]{1,0:T(8,128)S(1)}, u32[]{:S(2)}, u32[]{:S(2)}) collective-permute-start(f32[416,256]{1,0:T(8,128)} %bitcast.29), channel_id=1, source_target_pairs={{0,6},{1,25},{2,0},{3,27},{4,2},{5,29},{6,4},{7,31},{8,14},{9,1},{... | collective-permute-start | bytes 1277960 | tf_op jit(solution)/shard_map/ppermute | solution.py:55
  5.4 1.3 %collective-permute-start.31 = (f32[384,256]{1,0:T(8,128)}, f32[384,256]{1,0:T(8,128)S(1)}, u32[]{:S(2)}, u32[]{:S(2)}) collective-permute-start(f32[384,256]{1,0:T(8,128)} %bitcast.33), channel_id=1, source_target_pairs={{0,32},{32,64},{64,96},{96,0},{1,33},{33,65},{65,97},{97,1},{2,34}... | collective-permute-start | bytes 1179656 | tf_op jit(solution)/shard_map/ppermute | solution.py:438
  6.7 1.3 %collective-permute-start.32 = (s32[1,384]{1,0:T(1,128)}, s32[1,384]{1,0:T(1,128)S(1)}, u32[]{:S(2)}, u32[]{:S(2)}) collective-permute-start(s32[1,384]{1,0:T(1,128)} %param.10), channel_id=1, source_target_pairs={{0,32},{32,64},{64,96},{96,0},{1,33},{33,65},{65,97},{97,1},{2,34}... | collective-permute-start | bytes 4616 | tf_op jit(solution)/shard_map/ppermute | solution.py:439
  8.6 9.1 %collective-permute-done.32.dest_ref = s32[1,384]{1,0:T(1,128)S(1)} collective-permute-done((s32[1,384]{1,0:T(1,128)}, s32[1,384]{1,0:T(1,128)S(1)}, u32[]{:S(2)}, u32[]{:S(2)}) %collective-permute-start.32) | collective-permute-done | bytes 1568 | tf_op jit(solution)/shard_map/ppermute | solution.py:439
  18.2 2.1 %collective-permute-start.24 = (f32[416,256]{1,0:T(8,128)}, f32[416,256]{1,0:T(8,128)S(1)}, u32[]{:S(2)}, u32[]{:S(2)}) collective-permute-start(f32[416,256]{1,0:T(8,128)} %bitcast.32), channel_id=1, source_target_pairs={{0,24},{1,7},{2,26},{3,1},{4,28},{5,3},{6,30},{7,5},{8,0},{9,15},{... | collective-permute-start | bytes 1277960 | tf_op jit(solution)/shard_map/ppermute | solution.py:55
  20.3 1.3 %collective-permute-start.29 = (f32[416,256]{1,0:T(8,128)S(1)}, f32[416,256]{1,0:T(8,128)S(1)}, u32[]{:S(2)}, u32[]{:S(2)}) collective-permute-start(f32[416,256]{1,0:T(8,128)S(1)} %collective-permute-done.4.refs_4_), channel_id=1, source_target_pairs={{0,1},{1,0},{2,3},{3,2},{4,5},{5,4},{6,7},{7,6},{8,9},{9,8},{10,11... | collective-permute-start | bytes 1277960 | tf_op jit(solution)/shard_map/ppermute | solution.py:59
  21.8 4.6 %collective-permute-done.9.refs_3_ = f32[416,256]{1,0:T(8,128)S(1)} collective-permute-done((f32[416,256]{1,0:T(8,128)}, f32[416,256]{1,0:T(8,128)S(1)}, u32[]{:S(2)}, u32[]{:S(2)}) %collective-permute-start.9) | collective-permute-done | bytes 426016 | tf_op jit(solution)/shard_map/ppermute | solution.py:55
  26.4 3.5 %collective-permute-start.25 = (f32[416,256]{1,0:T(8,128)S(1)}, f32[416,256]{1,0:T(8,128)S(1)}, u32[]{:S(2)}, u32[]{:S(2)}) collective-permute-start(f32[416,256]{1,0:T(8,128)S(1)} %collective-permute-done.9.refs_3_), channel_id=1, source_target_pairs={{0,1},{1,0},{2,3},{3,2},{4,5},{5,4},{6,7},{7,6},{8,9},{9,8},{10,11... | collective-permute-start | bytes 1277960 | tf_op jit(solution)/shard_map/ppermute | solution.py:59
  29.9 0.8 copy-done.7
  30.7 1.0 collective-permute-start.15
  31.7 0.8 copy-done.9
  33.0 0.8 copy-done.3
  33.7 2.7 %collective-permute-start.14 = (f32[416,256]{1,0:T(8,128)S(1)}, f32[416,256]{1,0:T(8,128)}, u32[]{:S(2)}, u32[]{:S(2)}) collective-permute-start(f32[416,256]{1,0:T(8,128)S(1)} %collective-permute-done.refs_5_), channel_id=1, source_target_pairs={{0,24},{1,7},{2,26},{3,1},{4,28},{5,3},{6,30},{7,5},{8,0},{9,15},{... | collective-permute-start | bytes 1277960 | tf_op jit(solution)/shard_map/ppermute | solution.py:55
  36.4 0.8 copy-done.5
  37.2 0.8 collective-permute-done.15.refs_3_
  38.0 1.4 %collective-permute-start.27 = (f32[416,256]{1,0:T(8,128)}, f32[416,256]{1,0:T(8,128)}, u32[]{:S(2)}, u32[]{:S(2)}) collective-permute-start(f32[416,256]{1,0:T(8,128)} %collective-permute-done.5.refs_5_), channel_id=1, source_target_pairs={{0,1},{1,0},{2,3},{3,2},{4,5},{5,4},{6,7},{7,6},{8,9},{9,8},{10,11... | collective-permute-start | bytes 1277960 | tf_op jit(solution)/shard_map/ppermute | solution.py:59
  39.3 1.6 %collective-permute-done.1.refs_4_ = f32[416,256]{1,0:T(8,128)S(1)} collective-permute-done((f32[416,256]{1,0:T(8,128)S(1)}, f32[416,256]{1,0:T(8,128)S(1)}, u32[]{:S(2)}, u32[]{:S(2)}) %collective-permute-start.1) | collective-permute-done | bytes 426016 | tf_op jit(solution)/shard_map/ppermute | solution.py:55
  40.9 0.8 copy-done.1
  41.7 2.1 %collective-permute-start.21 = (f32[416,256]{1,0:T(8,128)S(1)}, f32[416,256]{1,0:T(8,128)}, u32[]{:S(2)}, u32[]{:S(2)}) collective-permute-start(f32[416,256]{1,0:T(8,128)S(1)} %collective-permute-done.15.refs_3_), channel_id=1, source_target_pairs={{0,1},{1,0},{2,3},{3,2},{4,5},{5,4},{6,7},{7,6},{8,9},{9,8},{10,11... | collective-permute-start | bytes 1277960 | tf_op jit(solution)/shard_map/ppermute | solution.py:59
  43.8 2.0 %shard_map.91 = f32[896,256]{1,0:T(8,128)} custom-call(f32[384,256]{1,0:T(8,128)S(1)} %collective-permute-done.31.rows_ref, s32[1,384]{1,0:T(1,128)S(1)} %collective-permute-done.32.dest_ref), custom_call_target="tpu_custom_call" | custom-call | flops 400000000 | bytes 2000000 | tf_op jit(solution)/shard_map/pallas_call | solution.py:122
  45.8 4.1 %all-to-all-start = ((f32[16,56,256]{2,1,0:T(8,128)}), f32[16,56,256]{2,1,0:T(8,128)S(1)}, u32[]{:S(2)}, u32[]{:S(2)}) async-start(f32[16,56,256]{2,1,0:T(8,128)} %bitcast.7), calls=%async_computation | async-start | bytes 1835008 | tf_op jit(solution)/shard_map/all_to_all | solution.py:441
  50.5 1.5 %collective-permute-start.2 = (f32[416,256]{1,0:T(8,128)}, f32[416,256]{1,0:T(8,128)}, u32[]{:S(2)}, u32[]{:S(2)}) collective-permute-start(f32[416,256]{1,0:T(8,128)} %copy-done.1), channel_id=1, source_target_pairs={{0,8},{1,3},{2,10},{3,5},{4,12},{5,7},{6,14},{7,1},{8,16},{9,11},{... | collective-permute-start | bytes 1277960 | tf_op jit(solution)/shard_map/ppermute | solution.py:55
  52.0 1.3 %collective-permute-start.16 = (f32[416,256]{1,0:T(8,128)S(1)}, f32[416,256]{1,0:T(8,128)}, u32[]{:S(2)}, u32[]{:S(2)}) collective-permute-start(f32[416,256]{1,0:T(8,128)S(1)} %collective-permute-done.15.refs_3_), channel_id=1, source_target_pairs={{0,24},{1,7},{2,26},{3,1},{4,28},{5,3},{6,30},{7,5},{8,0},{9,15},{... | collective-permute-start | bytes 1277960 | tf_op jit(solution)/shard_map/ppermute | solution.py:55
  53.3 2.2 %collective-permute-start.17 = (f32[416,256]{1,0:T(8,128)}, f32[416,256]{1,0:T(8,128)}, u32[]{:S(2)}, u32[]{:S(2)}) collective-permute-start(f32[416,256]{1,0:T(8,128)} %collective-permute-done.14.refs_3_), channel_id=1, source_target_pairs={{0,1},{1,0},{2,3},{3,2},{4,5},{5,4},{6,7},{7,6},{8,9},{9,8},{10,11... | collective-permute-start | bytes 1277960 | tf_op jit(solution)/shard_map/ppermute | solution.py:59
  56.2 2.5 %collective-permute-start.11 = (f32[416,256]{1,0:T(8,128)}, f32[416,256]{1,0:T(8,128)}, u32[]{:S(2)}, u32[]{:S(2)}) collective-permute-start(f32[416,256]{1,0:T(8,128)} %collective-permute-done.5.refs_5_), channel_id=1, source_target_pairs={{0,24},{1,7},{2,26},{3,1},{4,28},{5,3},{6,30},{7,5},{8,0},{9,15},{... | collective-permute-start | bytes 1277960 | tf_op jit(solution)/shard_map/ppermute | solution.py:55
  58.7 0.8 copy-done.13
  59.5 8.9 %collective-permute-done.2.refs_4_ = f32[416,256]{1,0:T(8,128)} collective-permute-done((f32[416,256]{1,0:T(8,128)}, f32[416,256]{1,0:T(8,128)}, u32[]{:S(2)}, u32[]{:S(2)}) %collective-permute-start.2) | collective-permute-done | bytes 426016 | tf_op jit(solution)/shard_map/ppermute | solution.py:55
  69.1 1.7 %collective-permute-start.3 = (f32[416,256]{1,0:T(8,128)}, f32[416,256]{1,0:T(8,128)}, u32[]{:S(2)}, u32[]{:S(2)}) collective-permute-start(f32[416,256]{1,0:T(8,128)} %collective-permute-done.2.refs_4_), channel_id=1, source_target_pairs={{0,6},{1,25},{2,0},{3,27},{4,2},{5,29},{6,4},{7,31},{8,14},{9,1},{... | collective-permute-start | bytes 1277960 | tf_op jit(solution)/shard_map/ppermute | solution.py:55
  72.2 1.0 copy-done.8
  73.2 1.0 copy-done.10
  74.2 4.3 %shard_map.86 = (f32[416,256]{1,0:T(8,128)S(1)}, f32[416,256]{1,0:T(8,128)S(1)}) custom-call(s32[3]{0:T(128)S(1)} %pad_add_fusion.refs_0_.where_ref, s32[1]{0:T(128)} %bitcast.13.refs_1_, f32[416,13312]{1,0:T(8,128)} %bitcast.22, f32[416,256]{1,0:T(8,128)S(1)} %collective-permute-done.28.refs_3_, f32[416,256]{1,0:T(8,128)S(1)} %collective-permute-done.4.refs_4_, ...), custom_call_target="tpu_custom_call" | custom-call | flops 1635778560 | bytes 6389760 | tf_op jit(solution)/shard_map/pallas_call | solution.py:262
  78.6 0.8 copy-done.15
  79.4 0.8 copy-done.18
  80.1 1.5 %shard_map.92 = (f32[416,256]{1,0:T(8,128)S(1)}, f32[416,256]{1,0:T(8,128)S(1)}) custom-call(s32[3]{0:T(128)S(1)} %pad_add_fusion.refs_0_.where_ref, f32[16,56,256]{2,1,0:T(8,128)S(1)} %all-to-all-done.in_ref), custom_call_target="tpu_custom_call" | custom-call | flops 400000000 | bytes 2000000 | tf_op jit(solution)/shard_map/pallas_call | solution.py:154
  82.3 1.0 copy-done.4
  83.3 1.0 copy-done.6
  84.3 1.0 copy-done.16
  85.3 5.3 %shard_map.87.refs_9_ = f32[416,256]{1,0:T(8,128)S(1)} custom-call(s32[3]{0:T(128)S(1)} %pad_add_fusion.refs_0_.where_ref, s32[1]{0:T(128)} %bitcast.14.refs_1_, f32[416,13312]{1,0:T(8,128)} %bitcast.23, f32[416,256]{1,0:T(8,128)S(1)} %collective-permute-done.9.refs_3_, f32[416,256]{1,0:T(8,128)S(1)} %collective-permute-done.24.refs_4_, ...), custom_call_target="tpu_custom_call" | custom-call | flops 1962934272 | bytes 7667712 | tf_op jit(solution)/shard_map/pallas_call | solution.py:262
  91.5 1.0 copy-done.2
  92.5 1.0 copy-done.12
  93.5 1.0 copy-done.14
  94.5 5.3 %shard_map.88.refs_9_ = f32[416,256]{1,0:T(8,128)S(1)} custom-call(s32[3]{0:T(128)S(1)} %pad_add_fusion.refs_0_.where_ref, s32[1]{0:T(128)} %bitcast.15.refs_1_, f32[416,13312]{1,0:T(8,128)} %bitcast.24, f32[416,256]{1,0:T(8,128)S(1)} %collective-permute-done.15.refs_3_, f32[416,256]{1,0:T(8,128)S(1)} %copy-done.2, ...), custom_call_target="tpu_custom_call" | custom-call | flops 1962934272 | bytes 7667712 | tf_op jit(solution)/shard_map/pallas_call | solution.py:262
  99.8 5.7 %shard_map.89.refs_7_ = f32[416,256]{1,0:T(8,128)S(1)} custom-call(s32[3]{0:T(128)S(1)} %pad_add_fusion.refs_0_.where_ref, s32[1]{0:T(128)} %bitcast.16.refs_1_, f32[416,13312]{1,0:T(8,128)} %bitcast.25, f32[416,256]{1,0:T(8,128)} %collective-permute-done.14.refs_3_, f32[416,256]{1,0:T(8,128)} %collective-permute-done.2.refs_4_, ...), custom_call_target="tpu_custom_call" | custom-call | flops 1962934272 | bytes 7667712 | tf_op jit(solution)/shard_map/pallas_call | solution.py:262
  105.6 4.4 %shard_map.90.refs_7_ = f32[416,256]{1,0:T(8,128)S(1)} custom-call(s32[3]{0:T(128)S(1)} %pad_add_fusion.refs_0_.where_ref, s32[1]{0:T(128)} %bitcast.17.refs_1_, f32[416,13312]{1,0:T(8,128)} %bitcast.26, f32[416,256]{1,0:T(8,128)} %collective-permute-done.10.refs_3_, f32[416,256]{1,0:T(8,128)} %collective-permute-done.11.refs_4_, ...), custom_call_target="tpu_custom_call" | custom-call | flops 1308622848 | bytes 5111808 | tf_op jit(solution)/shard_map/pallas_call | solution.py:262
  110.0 4.8 %shard_map.93 = (f32[416,256]{1,0:T(8,128)S(1)}, f32[128,256]{1,0:T(8,128)S(1)}) custom-call(s32[3]{0:T(128)S(1)} %pad_add_fusion.refs_0_.where_ref, s32[1]{0:T(128)} %bitcast.18.refs_1_, f32[416,13312]{1,0:T(8,128)} %bitcast.27, f32[416,256]{1,0:T(8,128)} %collective-permute-done.3.refs_3_, f32[416,256]{1,0:T(8,128)} %collective-permute-done.6.refs_4_, ...), custom_call_target="tpu_custom_call" | custom-call | flops 1308622848 | bytes 5111808 | tf_op jit(solution)/shard_map/pallas_call | solution.py:262
  115.3 1.1 collective-permute-done.34.sibling_ref
  116.4 8.4 %shard_map.94 = (f32[416,128]{1,0:T(8,128)}, f32[128,128]{1,0:T(8,128)}) custom-call(s32[3]{0:T(128)S(1)} %pad_add_fusion.refs_0_.where_ref, s32[1]{0:T(128)} %bitcast.19.rank_ref, f32[416,256]{1,0:T(8,128)S(1)} %get-tuple-element.13.sum_ref, f32[416,256]{1,0:T(8,128)S(1)} %copy-done.19, f32[128,256]{1,0:T(8,128)S(1)} %get-tuple-element.15.up_ref, ...), custom_call_target="tpu_custom_call" | custom-call | flops 2000000000 | bytes 2000000 | tf_op jit(solution)/shard_map/pallas_call | solution.py:410
  (75 shorter events, 6.7 us)
Async XLA Ops:
  0.6 114.7 %copy-start = (s32[1,16,128]{2,1,0:T(8,128)S(1)}, s32[1,16,128]{2,1,0:T(8,128)}, u32[]{:S(2)}) copy-start(s32[1,16,128]{2,1,0:T(8,128)} %param.13) | copy-start | bytes 24580
  0.6 19.7 %collective-permute-start.4 = (f32[416,256]{1,0:T(8,128)}, f32[416,256]{1,0:T(8,128)S(1)}, u32[]{:S(2)}, u32[]{:S(2)}) collective-permute-start(f32[416,256]{1,0:T(8,128)} %bitcast.28), channel_id=1, source_target_pairs={{0,2},{1,9},{2,4},{3,11},{4,6},{5,13},{6,0},{7,15},{8,10},{9,17},{... | collective-permute-start | bytes 1277960 | tf_op jit(solution)/shard_map/ppermute | solution.py:55
  3.2 18.5 %collective-permute-start = (f32[416,256]{1,0:T(8,128)}, f32[416,256]{1,0:T(8,128)S(1)}, u32[]{:S(2)}, u32[]{:S(2)}) collective-permute-start(f32[416,256]{1,0:T(8,128)} %bitcast.29), channel_id=1, source_target_pairs={{0,6},{1,25},{2,0},{3,27},{4,2},{5,29},{6,4},{7,31},{8,14},{9,1},{... | collective-permute-start | bytes 1277960 | tf_op jit(solution)/shard_map/ppermute | solution.py:55
  5.4 12.9 %collective-permute-start.31 = (f32[384,256]{1,0:T(8,128)}, f32[384,256]{1,0:T(8,128)S(1)}, u32[]{:S(2)}, u32[]{:S(2)}) collective-permute-start(f32[384,256]{1,0:T(8,128)} %bitcast.33), channel_id=1, source_target_pairs={{0,32},{32,64},{64,96},{96,0},{1,33},{33,65},{65,97},{97,1},{2,34}... | collective-permute-start | bytes 1179656 | tf_op jit(solution)/shard_map/ppermute | solution.py:438
  6.7 11.0 %collective-permute-start.32 = (s32[1,384]{1,0:T(1,128)}, s32[1,384]{1,0:T(1,128)S(1)}, u32[]{:S(2)}, u32[]{:S(2)}) collective-permute-start(s32[1,384]{1,0:T(1,128)} %param.10), channel_id=1, source_target_pairs={{0,32},{32,64},{64,96},{96,0},{1,33},{33,65},{65,97},{97,1},{2,34}... | collective-permute-start | bytes 4616 | tf_op jit(solution)/shard_map/ppermute | solution.py:439
  8.0 13.8 %collective-permute-start.28 = (f32[416,256]{1,0:T(8,128)}, f32[416,256]{1,0:T(8,128)S(1)}, u32[]{:S(2)}, u32[]{:S(2)}) collective-permute-start(f32[416,256]{1,0:T(8,128)} %bitcast.30), channel_id=1, source_target_pairs={{0,1},{1,0},{2,3},{3,2},{4,5},{5,4},{6,7},{7,6},{8,9},{9,8},{10,11... | collective-permute-start | bytes 1277960 | tf_op jit(solution)/shard_map/ppermute | solution.py:59
  17.7 8.7 %collective-permute-start.9 = (f32[416,256]{1,0:T(8,128)}, f32[416,256]{1,0:T(8,128)S(1)}, u32[]{:S(2)}, u32[]{:S(2)}) collective-permute-start(f32[416,256]{1,0:T(8,128)} %bitcast.31), channel_id=1, source_target_pairs={{0,8},{1,3},{2,10},{3,5},{4,12},{5,7},{6,14},{7,1},{8,16},{9,11},{... | collective-permute-start | bytes 1277960 | tf_op jit(solution)/shard_map/ppermute | solution.py:55
  18.2 11.7 %collective-permute-start.24 = (f32[416,256]{1,0:T(8,128)}, f32[416,256]{1,0:T(8,128)S(1)}, u32[]{:S(2)}, u32[]{:S(2)}) collective-permute-start(f32[416,256]{1,0:T(8,128)} %bitcast.32), channel_id=1, source_target_pairs={{0,24},{1,7},{2,26},{3,1},{4,28},{5,3},{6,30},{7,5},{8,0},{9,15},{... | collective-permute-start | bytes 1277960 | tf_op jit(solution)/shard_map/ppermute | solution.py:55
  20.3 9.6 %collective-permute-start.29 = (f32[416,256]{1,0:T(8,128)S(1)}, f32[416,256]{1,0:T(8,128)S(1)}, u32[]{:S(2)}, u32[]{:S(2)}) collective-permute-start(f32[416,256]{1,0:T(8,128)S(1)} %collective-permute-done.4.refs_4_), channel_id=1, source_target_pairs={{0,1},{1,0},{2,3},{3,2},{4,5},{5,4},{6,7},{7,6},{8,9},{9,8},{10,11... | collective-permute-start | bytes 1277960 | tf_op jit(solution)/shard_map/ppermute | solution.py:59
  21.7 10.0 %collective-permute-start.30 = (f32[416,256]{1,0:T(8,128)S(1)}, f32[416,256]{1,0:T(8,128)S(1)}, u32[]{:S(2)}, u32[]{:S(2)}) collective-permute-start(f32[416,256]{1,0:T(8,128)S(1)} %collective-permute-done.refs_5_), channel_id=1, source_target_pairs={{0,1},{1,0},{2,3},{3,2},{4,5},{5,4},{6,7},{7,6},{8,9},{9,8},{10,11... | collective-permute-start | bytes 1277960 | tf_op jit(solution)/shard_map/ppermute | solution.py:59
  21.8 11.2 %collective-permute-start.5 = (f32[416,256]{1,0:T(8,128)S(1)}, f32[416,256]{1,0:T(8,128)}, u32[]{:S(2)}, u32[]{:S(2)}) collective-permute-start(f32[416,256]{1,0:T(8,128)S(1)} %collective-permute-done.4.refs_4_), channel_id=1, source_target_pairs={{0,2},{1,9},{2,4},{3,11},{4,6},{5,13},{6,0},{7,15},{8,10},{9,17},{... | collective-permute-start | bytes 1277960 | tf_op jit(solution)/shard_map/ppermute | solution.py:55
  26.4 6.6 %collective-permute-start.25 = (f32[416,256]{1,0:T(8,128)S(1)}, f32[416,256]{1,0:T(8,128)S(1)}, u32[]{:S(2)}, u32[]{:S(2)}) collective-permute-start(f32[416,256]{1,0:T(8,128)S(1)} %collective-permute-done.9.refs_3_), channel_id=1, source_target_pairs={{0,1},{1,0},{2,3},{3,2},{4,5},{5,4},{6,7},{7,6},{8,9},{9,8},{10,11... | collective-permute-start | bytes 1277960 | tf_op jit(solution)/shard_map/ppermute | solution.py:59
  29.9 6.5 %collective-permute-start.26 = (f32[416,256]{1,0:T(8,128)S(1)}, f32[416,256]{1,0:T(8,128)S(1)}, u32[]{:S(2)}, u32[]{:S(2)}) collective-permute-start(f32[416,256]{1,0:T(8,128)S(1)} %collective-permute-done.24.refs_4_), channel_id=1, source_target_pairs={{0,1},{1,0},{2,3},{3,2},{4,5},{5,4},{6,7},{7,6},{8,9},{9,8},{10,11... | collective-permute-start | bytes 1277960 | tf_op jit(solution)/shard_map/ppermute | solution.py:59
  30.7 7.3 %collective-permute-start.15 = (f32[416,256]{1,0:T(8,128)S(1)}, f32[416,256]{1,0:T(8,128)S(1)}, u32[]{:S(2)}, u32[]{:S(2)}) collective-permute-start(f32[416,256]{1,0:T(8,128)S(1)} %collective-permute-done.4.refs_4_), channel_id=1, source_target_pairs={{0,24},{1,7},{2,26},{3,1},{4,28},{5,3},{6,30},{7,5},{8,0},{9,15},{... | collective-permute-start | bytes 1277960 | tf_op jit(solution)/shard_map/ppermute | solution.py:55
  32.5 8.5 %collective-permute-start.1 = (f32[416,256]{1,0:T(8,128)S(1)}, f32[416,256]{1,0:T(8,128)S(1)}, u32[]{:S(2)}, u32[]{:S(2)}) collective-permute-start(f32[416,256]{1,0:T(8,128)S(1)} %collective-permute-done.refs_5_), channel_id=1, source_target_pairs={{0,8},{1,3},{2,10},{3,5},{4,12},{5,7},{6,14},{7,1},{8,16},{9,11},{... | collective-permute-start | bytes 1277960 | tf_op jit(solution)/shard_map/ppermute | solution.py:55
  33.0 16.9 %collective-permute-start.20 = (f32[416,256]{1,0:T(8,128)S(1)}, f32[416,256]{1,0:T(8,128)}, u32[]{:S(2)}, u32[]{:S(2)}) collective-permute-start(f32[416,256]{1,0:T(8,128)S(1)} %collective-permute-done.4.refs_4_), channel_id=1, source_target_pairs={{0,8},{1,3},{2,10},{3,5},{4,12},{5,7},{6,14},{7,1},{8,16},{9,11},{... | collective-permute-start | bytes 1277960 | tf_op jit(solution)/shard_map/ppermute | solution.py:55
  33.7 16.5 %collective-permute-start.14 = (f32[416,256]{1,0:T(8,128)S(1)}, f32[416,256]{1,0:T(8,128)}, u32[]{:S(2)}, u32[]{:S(2)}) collective-permute-start(f32[416,256]{1,0:T(8,128)S(1)} %collective-permute-done.refs_5_), channel_id=1, source_target_pairs={{0,24},{1,7},{2,26},{3,1},{4,28},{5,3},{6,30},{7,5},{8,0},{9,15},{... | collective-permute-start | bytes 1277960 | tf_op jit(solution)/shard_map/ppermute | solution.py:55
  37.2 13.3 %collective-permute-start.10 = (f32[416,256]{1,0:T(8,128)S(1)}, f32[416,256]{1,0:T(8,128)}, u32[]{:S(2)}, u32[]{:S(2)}) collective-permute-start(f32[416,256]{1,0:T(8,128)S(1)} %collective-permute-done.9.refs_3_), channel_id=1, source_target_pairs={{0,8},{1,3},{2,10},{3,5},{4,12},{5,7},{6,14},{7,1},{8,16},{9,11},{... | collective-permute-start | bytes 1277960 | tf_op jit(solution)/shard_map/ppermute | solution.py:55
  38.0 14.1 %collective-permute-start.27 = (f32[416,256]{1,0:T(8,128)}, f32[416,256]{1,0:T(8,128)}, u32[]{:S(2)}, u32[]{:S(2)}) collective-permute-start(f32[416,256]{1,0:T(8,128)} %collective-permute-done.5.refs_5_), channel_id=1, source_target_pairs={{0,1},{1,0},{2,3},{3,2},{4,5},{5,4},{6,7},{7,6},{8,9},{9,8},{10,11... | collective-permute-start | bytes 1277960 | tf_op jit(solution)/shard_map/ppermute | solution.py:59
  41.7 11.6 %collective-permute-start.21 = (f32[416,256]{1,0:T(8,128)S(1)}, f32[416,256]{1,0:T(8,128)}, u32[]{:S(2)}, u32[]{:S(2)}) collective-permute-start(f32[416,256]{1,0:T(8,128)S(1)} %collective-permute-done.15.refs_3_), channel_id=1, source_target_pairs={{0,1},{1,0},{2,3},{3,2},{4,5},{5,4},{6,7},{7,6},{8,9},{9,8},{10,11... | collective-permute-start | bytes 1277960 | tf_op jit(solution)/shard_map/ppermute | solution.py:59
  45.8 34.4 %all-to-all-start = ((f32[16,56,256]{2,1,0:T(8,128)}), f32[16,56,256]{2,1,0:T(8,128)S(1)}, u32[]{:S(2)}, u32[]{:S(2)}) async-start(f32[16,56,256]{2,1,0:T(8,128)} %bitcast.7), calls=%async_computation | async-start | bytes 1835008 | tf_op jit(solution)/shard_map/all_to_all | solution.py:441
  49.9 5.6 %collective-permute-start.22 = (f32[416,256]{1,0:T(8,128)}, f32[416,256]{1,0:T(8,128)S(1)}, u32[]{:S(2)}, u32[]{:S(2)}) collective-permute-start(f32[416,256]{1,0:T(8,128)} %copy-done.1), channel_id=1, source_target_pairs={{0,1},{1,0},{2,3},{3,2},{4,5},{5,4},{6,7},{7,6},{8,9},{9,8},{10,11... | collective-permute-start | bytes 1277960 | tf_op jit(solution)/shard_map/ppermute | solution.py:59
  50.3 8.4 %collective-permute-start.23 = (f32[416,256]{1,0:T(8,128)}, f32[416,256]{1,0:T(8,128)S(1)}, u32[]{:S(2)}, u32[]{:S(2)}) collective-permute-start(f32[416,256]{1,0:T(8,128)} %collective-permute-done.20.refs_5_), channel_id=1, source_target_pairs={{0,1},{1,0},{2,3},{3,2},{4,5},{5,4},{6,7},{7,6},{8,9},{9,8},{10,11... | collective-permute-start | bytes 1277960 | tf_op jit(solution)/shard_map/ppermute | solution.py:59
  50.5 17.9 %collective-permute-start.2 = (f32[416,256]{1,0:T(8,128)}, f32[416,256]{1,0:T(8,128)}, u32[]{:S(2)}, u32[]{:S(2)}) collective-permute-start(f32[416,256]{1,0:T(8,128)} %copy-done.1), channel_id=1, source_target_pairs={{0,8},{1,3},{2,10},{3,5},{4,12},{5,7},{6,14},{7,1},{8,16},{9,11},{... | collective-permute-start | bytes 1277960 | tf_op jit(solution)/shard_map/ppermute | solution.py:55
  52.0 17.1 %collective-permute-start.16 = (f32[416,256]{1,0:T(8,128)S(1)}, f32[416,256]{1,0:T(8,128)}, u32[]{:S(2)}, u32[]{:S(2)}) collective-permute-start(f32[416,256]{1,0:T(8,128)S(1)} %collective-permute-done.15.refs_3_), channel_id=1, source_target_pairs={{0,24},{1,7},{2,26},{3,1},{4,28},{5,3},{6,30},{7,5},{8,0},{9,15},{... | collective-permute-start | bytes 1277960 | tf_op jit(solution)/shard_map/ppermute | solution.py:55
  53.3 17.5 %collective-permute-start.17 = (f32[416,256]{1,0:T(8,128)}, f32[416,256]{1,0:T(8,128)}, u32[]{:S(2)}, u32[]{:S(2)}) collective-permute-start(f32[416,256]{1,0:T(8,128)} %collective-permute-done.14.refs_3_), channel_id=1, source_target_pairs={{0,1},{1,0},{2,3},{3,2},{4,5},{5,4},{6,7},{7,6},{8,9},{9,8},{10,11... | collective-permute-start | bytes 1277960 | tf_op jit(solution)/shard_map/ppermute | solution.py:59
  56.2 25.5 %collective-permute-start.11 = (f32[416,256]{1,0:T(8,128)}, f32[416,256]{1,0:T(8,128)}, u32[]{:S(2)}, u32[]{:S(2)}) collective-permute-start(f32[416,256]{1,0:T(8,128)} %collective-permute-done.5.refs_5_), channel_id=1, source_target_pairs={{0,24},{1,7},{2,26},{3,1},{4,28},{5,3},{6,30},{7,5},{8,0},{9,15},{... | collective-permute-start | bytes 1277960 | tf_op jit(solution)/shard_map/ppermute | solution.py:55
  58.7 0.8 copy-start.13
  59.5 22.3 %collective-permute-start.6 = (f32[416,256]{1,0:T(8,128)}, f32[416,256]{1,0:T(8,128)}, u32[]{:S(2)}, u32[]{:S(2)}) collective-permute-start(f32[416,256]{1,0:T(8,128)} %collective-permute-done.5.refs_5_), channel_id=1, source_target_pairs={{0,8},{1,3},{2,10},{3,5},{4,12},{5,7},{6,14},{7,1},{8,16},{9,11},{... | collective-permute-start | bytes 1277960 | tf_op jit(solution)/shard_map/ppermute | solution.py:55
  68.4 22.2 %collective-permute-start.18 = (f32[416,256]{1,0:T(8,128)}, f32[416,256]{1,0:T(8,128)}, u32[]{:S(2)}, u32[]{:S(2)}) collective-permute-start(f32[416,256]{1,0:T(8,128)} %collective-permute-done.2.refs_4_), channel_id=1, source_target_pairs={{0,1},{1,0},{2,3},{3,2},{4,5},{5,4},{6,7},{7,6},{8,9},{9,8},{10,11... | collective-permute-start | bytes 1277960 | tf_op jit(solution)/shard_map/ppermute | solution.py:59
  69.1 22.1 %collective-permute-start.3 = (f32[416,256]{1,0:T(8,128)}, f32[416,256]{1,0:T(8,128)}, u32[]{:S(2)}, u32[]{:S(2)}) collective-permute-start(f32[416,256]{1,0:T(8,128)} %collective-permute-done.2.refs_4_), channel_id=1, source_target_pairs={{0,6},{1,25},{2,0},{3,27},{4,2},{5,29},{6,4},{7,31},{8,14},{9,1},{... | collective-permute-start | bytes 1277960 | tf_op jit(solution)/shard_map/ppermute | solution.py:55
  70.8 20.0 %collective-permute-start.19 = (f32[416,256]{1,0:T(8,128)}, f32[416,256]{1,0:T(8,128)}, u32[]{:S(2)}, u32[]{:S(2)}) collective-permute-start(f32[416,256]{1,0:T(8,128)} %collective-permute-done.16.refs_5_), channel_id=1, source_target_pairs={{0,1},{1,0},{2,3},{3,2},{4,5},{5,4},{6,7},{7,6},{8,9},{9,8},{10,11... | collective-permute-start | bytes 1277960 | tf_op jit(solution)/shard_map/ppermute | solution.py:59
  72.2 1.0 copy-start.8
  73.2 1.0 copy-start.10
  81.7 23.8 %collective-permute-start.12 = (f32[416,256]{1,0:T(8,128)}, f32[416,256]{1,0:T(8,128)S(1)}, u32[]{:S(2)}, u32[]{:S(2)}) collective-permute-start(f32[416,256]{1,0:T(8,128)} %collective-permute-done.10.refs_3_), channel_id=1, source_target_pairs={{0,1},{1,0},{2,3},{3,2},{4,5},{5,4},{6,7},{7,6},{8,9},{9,8},{10,11... | collective-permute-start | bytes 1277960 | tf_op jit(solution)/shard_map/ppermute | solution.py:59
  81.8 23.7 %collective-permute-start.13 = (f32[416,256]{1,0:T(8,128)}, f32[416,256]{1,0:T(8,128)S(1)}, u32[]{:S(2)}, u32[]{:S(2)}) collective-permute-start(f32[416,256]{1,0:T(8,128)} %collective-permute-done.11.refs_4_), channel_id=1, source_target_pairs={{0,1},{1,0},{2,3},{3,2},{4,5},{5,4},{6,7},{7,6},{8,9},{9,8},{10,11... | collective-permute-start | bytes 1277960 | tf_op jit(solution)/shard_map/ppermute | solution.py:59
  82.3 1.0 copy-start.4
  83.3 1.0 copy-start.6
  84.3 1.0 copy-start.16
  90.6 19.3 %collective-permute-start.33 = (f32[416,256]{1,0:T(8,128)S(1)}, f32[416,256]{1,0:T(8,128)S(1)}, u32[]{:S(2)}, u32[]{:S(2)}) collective-permute-start(f32[416,256]{1,0:T(8,128)S(1)} %get-tuple-element.12), channel_id=1, source_target_pairs={{0,1},{1,0},{2,3},{3,2},{4,5},{5,4},{6,7},{7,6},{8,9},{9,8},{10,11... | collective-permute-start | bytes 1277960 | tf_op jit(solution)/shard_map/ppermute | solution.py:59
  90.8 19.2 %collective-permute-start.8 = (f32[416,256]{1,0:T(8,128)}, f32[416,256]{1,0:T(8,128)S(1)}, u32[]{:S(2)}, u32[]{:S(2)}) collective-permute-start(f32[416,256]{1,0:T(8,128)} %collective-permute-done.6.refs_4_), channel_id=1, source_target_pairs={{0,1},{1,0},{2,3},{3,2},{4,5},{5,4},{6,7},{7,6},{8,9},{9,8},{10,11... | collective-permute-start | bytes 1277960 | tf_op jit(solution)/shard_map/ppermute | solution.py:59
  91.2 18.7 %collective-permute-start.7 = (f32[416,256]{1,0:T(8,128)}, f32[416,256]{1,0:T(8,128)S(1)}, u32[]{:S(2)}, u32[]{:S(2)}) collective-permute-start(f32[416,256]{1,0:T(8,128)} %collective-permute-done.3.refs_3_), channel_id=1, source_target_pairs={{0,1},{1,0},{2,3},{3,2},{4,5},{5,4},{6,7},{7,6},{8,9},{9,8},{10,11... | collective-permute-start | bytes 1277960 | tf_op jit(solution)/shard_map/ppermute | solution.py:59
  91.5 1.0 copy-start.2
  92.5 1.0 copy-start.12
  93.5 1.0 copy-start.14
  99.8 10.2 %copy-start.17 = (s32[1,1,128]{2,1,0:T(1,128)S(1)}, s32[1,1,128]{2,1,0:T(1,128)}, u32[]{:S(2)}) copy-start(s32[1,1,128]{2,1,0:T(1,128)} %param.11) | copy-start | bytes 1540
  105.5 10.9 %copy-start.19 = (f32[416,256]{1,0:T(8,128)S(1)}, f32[416,256]{1,0:T(8,128)}, u32[]{:S(2)}) copy-start(f32[416,256]{1,0:T(8,128)} %copy-done.18) | copy-start | bytes 1277956
  114.7 1.7 %collective-permute-start.34 = (f32[128,256]{1,0:T(8,128)S(1)}, f32[128,256]{1,0:T(8,128)S(1)}, u32[]{:S(2)}, u32[]{:S(2)}) collective-permute-start(f32[128,256]{1,0:T(8,128)S(1)} %get-tuple-element.15.up_ref), channel_id=1, source_target_pairs={{0,1},{1,0},{2,3},{3,2},{4,5},{5,4},{6,7},{7,6},{8,9},{9,8},{10,11... | collective-permute-start | bytes 393224 | tf_op jit(solution)/shard_map/ppermute | solution.py:59
  (8 other events, 6.2 us)

commit v2 on v1

--- a/solution.py
+++ b/solution.py
@@ -36,8 +36,7 @@
     ((1, 0), (3, 0)),
     ((0, 1), (0, 3), (2, 0)),
     ((1, 3), (3, 1), (1, 1)),
-    ((3, 3), (3, 2), (1, 2)),
-    ((0, 2), (2, 3)),
+    ((3, 3), (3, 2), (1, 2), (0, 2), (2, 3)),
     ((2, 2), (2, 1)),
 )
 
@@ -122,7 +121,7 @@
     return pl.pallas_call(
         pack_kernel,
         out_shape=jax.ShapeDtypeStruct((16 * GROUP, SAMPLES), f32),
-        compiler_params=pltpu.CompilerParams(vmem_limit_bytes=24 * 1024 * 1024),
+        compiler_params=pltpu.CompilerParams(vmem_limit_bytes=12 * 1024 * 1024),
         cost_estimate=pl.CostEstimate(flops=400_000_000, bytes_accessed=2_000_000, transcendentals=0),
     )(rows, dest)
 
@@ -157,7 +156,7 @@
         in_specs=[pl.BlockSpec(memory_space=pltpu.SMEM), vmem],
         out_specs=(vmem, vmem),
         scratch_shapes=[pltpu.VMEM((128, 128), f32)],
-        compiler_params=pltpu.CompilerParams(vmem_limit_bytes=24 * 1024 * 1024),
+        compiler_params=pltpu.CompilerParams(vmem_limit_bytes=12 * 1024 * 1024),
         cost_estimate=pl.CostEstimate(flops=400_000_000, bytes_accessed=2_000_000, transcendentals=0),
     )(where, arrived)
 
@@ -416,7 +415,7 @@
         in_specs=[smem, smem] + [vmem] * 6,
         out_specs=(vmem, vmem),
         scratch_shapes=[pltpu.VMEM((2, RANK, RANK), f32)],
-        compiler_params=pltpu.CompilerParams(vmem_limit_bytes=24 * 1024 * 1024),
+        compiler_params=pltpu.CompilerParams(vmem_limit_bytes=12 * 1024 * 1024),
         cost_estimate=pl.CostEstimate(flops=2_000_000_000, bytes_accessed=2_000_000, transcendentals=0),
     )(where, rank, total, near, upward, sibling, chosen, pick)
 

time: 125 us -> 127 us (1.016)
  waiting for transfers between devices: 26.1 us -> 32.7 us
  local copies, waits for them, and re-layouts: 15.1 us -> 9.66 us
  starting transfers between devices: 40.4 us -> 43.1 us
  Pallas kernels: 41.6 us -> 40 us
    ppermute x15, waiting for transfers between devices: 15.9 us -> 22.5 us  [chips_step(): return lax.ppermute(value, BLK, pairs)]
    unnamed x40 -> x32, local copies, waits for them, and re-layouts: 15.1 us -> 9.66 us
    ppermute x15, starting transfers between devices: 18.6 us -> 20.5 us  [chips_step(): return lax.ppermute(value, BLK, pairs)]
    pallas_call x6 -> x5, Pallas kernels: 29.7 us -> 28 us  [product(): pl.pallas_call(kernel, out_shape=tuple(out_shape), in_specs=specs, out_sp...]
  transfers between devices with their start and end apart: 36 -> 36, of which waited for: 6 -> 8; matrix products, arithmetic and copies ran while one was open for 0% -> 0% of each run, Pallas kernels for 23% -> 21%
where the time goes in v2:
time: 127 us
  starting transfers between devices  43.1 us (34%)
  Pallas kernels  40 us (31%)
  waiting for transfers between devices  32.7 us (26%)
  local copies, waits for them, and re-layouts  9.66 us (8%)
  between operations  1.51 us (1%)
    pallas_call x5, Pallas kernels, product(): pl.pallas_call(kernel, out_shape=tuple(out_shape), in_specs=specs, out_sp...  28 us
    ppermute x15, waiting for transfers between devices, chips_step(): return lax.ppermute(value, BLK, pairs)  22.5 us
    ppermute x15, starting transfers between devices, chips_step(): return lax.ppermute(value, BLK, pairs)  20.5 us
    ppermute x18, starting transfers between devices, swap_cores(): return lax.ppermute(value, 'blk_2', [(0, 1), (1, 0)])  15.8 us
    unnamed x32, local copies, waits for them, and re-layouts  9.66 us
    ppermute x1, waiting for transfers between devices, body(): dest = lax.ppermute(child_dest, 'front', ahead)  9.06 us
    pallas_call x1, Pallas kernels, finish(): pl.pallas_call(finish_kernel, out_shape=(jax.ShapeDtypeStruct((HEIGHT, RA...  8.4 us
    all_to_all x1, starting transfers between devices, body(): arrived = lax.all_to_all(sending, ('blk_0', 'blk_1'), 0, 0, tiled=True)  4.12 us
  transfers between devices with their start and end apart: 36, of which 8 were waited for; matrix products, arithmetic and copies ran while one was open for 0% of the time, Pallas kernels for 21%

profile of v2, /device:TPU:1, one launch (start us, length us, event | category | flops | bytes accessed | tf_op | source)
XLA Modules:
  0.0 127.0 jit_solution(12328699737823217765)
XLA Ops:
  0.6 2.5 %collective-permute-start.4 = (f32[416,256]{1,0:T(8,128)}, f32[416,256]{1,0:T(8,128)S(1)}, u32[]{:S(2)}, u32[]{:S(2)}) collective-permute-start(f32[416,256]{1,0:T(8,128)} %bitcast.26), channel_id=1, source_target_pairs={{0,2},{1,9},{2,4},{3,11},{4,6},{5,13},{6,0},{7,15},{8,10},{9,17},{... | collective-permute-start | bytes 1277960 | tf_op jit(solution)/shard_map/ppermute | solution.py:54
  3.2 2.2 %collective-permute-start = (f32[416,256]{1,0:T(8,128)}, f32[416,256]{1,0:T(8,128)S(1)}, u32[]{:S(2)}, u32[]{:S(2)}) collective-permute-start(f32[416,256]{1,0:T(8,128)} %bitcast.27), channel_id=1, source_target_pairs={{0,6},{1,25},{2,0},{3,27},{4,2},{5,29},{6,4},{7,31},{8,14},{9,1},{... | collective-permute-start | bytes 1277960 | tf_op jit(solution)/shard_map/ppermute | solution.py:54
  5.4 1.3 %collective-permute-start.31 = (f32[384,256]{1,0:T(8,128)}, f32[384,256]{1,0:T(8,128)S(1)}, u32[]{:S(2)}, u32[]{:S(2)}) collective-permute-start(f32[384,256]{1,0:T(8,128)} %bitcast.31), channel_id=1, source_target_pairs={{0,32},{32,64},{64,96},{96,0},{1,33},{33,65},{65,97},{97,1},{2,34}... | collective-permute-start | bytes 1179656 | tf_op jit(solution)/shard_map/ppermute | solution.py:437
  6.7 1.3 %collective-permute-start.32 = (s32[1,384]{1,0:T(1,128)}, s32[1,384]{1,0:T(1,128)S(1)}, u32[]{:S(2)}, u32[]{:S(2)}) collective-permute-start(s32[1,384]{1,0:T(1,128)} %param.10), channel_id=1, source_target_pairs={{0,32},{32,64},{64,96},{96,0},{1,33},{33,65},{65,97},{97,1},{2,34}... | collective-permute-start | bytes 4616 | tf_op jit(solution)/shard_map/ppermute | solution.py:438
  8.0 0.6 collective-permute-start.28
  8.6 9.1 %collective-permute-done.32.dest_ref = s32[1,384]{1,0:T(1,128)S(1)} collective-permute-done((s32[1,384]{1,0:T(1,128)}, s32[1,384]{1,0:T(1,128)S(1)}, u32[]{:S(2)}, u32[]{:S(2)}) %collective-permute-start.32) | collective-permute-done | bytes 1568 | tf_op jit(solution)/shard_map/ppermute | solution.py:438
  18.2 2.1 %collective-permute-start.24 = (f32[416,256]{1,0:T(8,128)}, f32[416,256]{1,0:T(8,128)S(1)}, u32[]{:S(2)}, u32[]{:S(2)}) collective-permute-start(f32[416,256]{1,0:T(8,128)} %bitcast.30), channel_id=1, source_target_pairs={{0,24},{1,7},{2,26},{3,1},{4,28},{5,3},{6,30},{7,5},{8,0},{9,15},{... | collective-permute-start | bytes 1277960 | tf_op jit(solution)/shard_map/ppermute | solution.py:54
  20.3 1.3 %collective-permute-start.29 = (f32[416,256]{1,0:T(8,128)S(1)}, f32[416,256]{1,0:T(8,128)S(1)}, u32[]{:S(2)}, u32[]{:S(2)}) collective-permute-start(f32[416,256]{1,0:T(8,128)S(1)} %collective-permute-done.4.refs_4_), channel_id=1, source_target_pairs={{0,1},{1,0},{2,3},{3,2},{4,5},{5,4},{6,7},{7,6},{8,9},{9,8},{10,11... | collective-permute-start | bytes 1277960 | tf_op jit(solution)/shard_map/ppermute | solution.py:58
  21.8 4.6 %collective-permute-done.12.refs_3_ = f32[416,256]{1,0:T(8,128)S(1)} collective-permute-done((f32[416,256]{1,0:T(8,128)}, f32[416,256]{1,0:T(8,128)S(1)}, u32[]{:S(2)}, u32[]{:S(2)}) %collective-permute-start.12) | collective-permute-done | bytes 426016 | tf_op jit(solution)/shard_map/ppermute | solution.py:54
  26.4 3.5 %collective-permute-start.25 = (f32[416,256]{1,0:T(8,128)S(1)}, f32[416,256]{1,0:T(8,128)S(1)}, u32[]{:S(2)}, u32[]{:S(2)}) collective-permute-start(f32[416,256]{1,0:T(8,128)S(1)} %collective-permute-done.12.refs_3_), channel_id=1, source_target_pairs={{0,1},{1,0},{2,3},{3,2},{4,5},{5,4},{6,7},{7,6},{8,9},{9,8},{10,11... | collective-permute-start | bytes 1277960 | tf_op jit(solution)/shard_map/ppermute | solution.py:58
  29.9 1.0 collective-permute-start.10
  31.0 0.8 copy-done.5
  32.2 0.8 copy-done.7
  33.0 2.7 %collective-permute-start.9 = (f32[416,256]{1,0:T(8,128)S(1)}, f32[416,256]{1,0:T(8,128)S(1)}, u32[]{:S(2)}, u32[]{:S(2)}) collective-permute-start(f32[416,256]{1,0:T(8,128)S(1)} %collective-permute-done.refs_5_), channel_id=1, source_target_pairs={{0,24},{1,7},{2,26},{3,1},{4,28},{5,3},{6,30},{7,5},{8,0},{9,15},{... | collective-permute-start | bytes 1277960 | tf_op jit(solution)/shard_map/ppermute | solution.py:54
  35.7 0.8 copy-done.9
  36.5 0.9 collective-permute-done.10.refs_3_
  37.4 1.2 collective-permute-start.27
  38.5 1.8 %collective-permute-done.1.refs_4_ = f32[416,256]{1,0:T(8,128)} collective-permute-done((f32[416,256]{1,0:T(8,128)S(1)}, f32[416,256]{1,0:T(8,128)}, u32[]{:S(2)}, u32[]{:S(2)}) %collective-permute-start.1) | collective-permute-done | bytes 426016 | tf_op jit(solution)/shard_map/ppermute | solution.py:54
  40.3 2.0 %collective-permute-start.21 = (f32[416,256]{1,0:T(8,128)S(1)}, f32[416,256]{1,0:T(8,128)}, u32[]{:S(2)}, u32[]{:S(2)}) collective-permute-start(f32[416,256]{1,0:T(8,128)S(1)} %collective-permute-done.10.refs_3_), channel_id=1, source_target_pairs={{0,1},{1,0},{2,3},{3,2},{4,5},{5,4},{6,7},{7,6},{8,9},{9,8},{10,11... | collective-permute-start | bytes 1277960 | tf_op jit(solution)/shard_map/ppermute | solution.py:58
  42.3 2.6 %collective-permute-done.20.refs_5_ = f32[416,256]{1,0:T(8,128)} collective-permute-done((f32[416,256]{1,0:T(8,128)S(1)}, f32[416,256]{1,0:T(8,128)}, u32[]{:S(2)}, u32[]{:S(2)}) %collective-permute-start.20) | collective-permute-done | bytes 426016 | tf_op jit(solution)/shard_map/ppermute | solution.py:54
  44.9 2.0 %collective-permute-start.22 = (f32[416,256]{1,0:T(8,128)}, f32[416,256]{1,0:T(8,128)}, u32[]{:S(2)}, u32[]{:S(2)}) collective-permute-start(f32[416,256]{1,0:T(8,128)} %collective-permute-done.1.refs_4_), channel_id=1, source_target_pairs={{0,1},{1,0},{2,3},{3,2},{4,5},{5,4},{6,7},{7,6},{8,9},{9,8},{10,11... | collective-permute-start | bytes 1277960 | tf_op jit(solution)/shard_map/ppermute | solution.py:58
  46.8 0.8 copy-done.3
  47.6 2.0 %shard_map.90 = f32[896,256]{1,0:T(8,128)} custom-call(f32[384,256]{1,0:T(8,128)S(1)} %collective-permute-done.31.rows_ref, s32[1,384]{1,0:T(1,128)S(1)} %collective-permute-done.32.dest_ref), custom_call_target="tpu_custom_call" | custom-call | flops 400000000 | bytes 2000000 | tf_op jit(solution)/shard_map/pallas_call | solution.py:121
  49.6 4.1 %all-to-all-start = ((f32[16,56,256]{2,1,0:T(8,128)}), f32[16,56,256]{2,1,0:T(8,128)S(1)}, u32[]{:S(2)}, u32[]{:S(2)}) async-start(f32[16,56,256]{2,1,0:T(8,128)} %bitcast.7), calls=%async_computation | async-start | bytes 1835008 | tf_op jit(solution)/shard_map/all_to_all | solution.py:440
  53.8 2.6 %collective-permute-start.14 = (f32[416,256]{1,0:T(8,128)}, f32[416,256]{1,0:T(8,128)}, u32[]{:S(2)}, u32[]{:S(2)}) collective-permute-start(f32[416,256]{1,0:T(8,128)} %collective-permute-done.5.refs_5_), channel_id=1, source_target_pairs={{0,24},{1,7},{2,26},{3,1},{4,28},{5,3},{6,30},{7,5},{8,0},{9,15},{... | collective-permute-start | bytes 1277960 | tf_op jit(solution)/shard_map/ppermute | solution.py:54
  56.4 2.7 %collective-permute-start.11 = (f32[416,256]{1,0:T(8,128)S(1)}, f32[416,256]{1,0:T(8,128)}, u32[]{:S(2)}, u32[]{:S(2)}) collective-permute-start(f32[416,256]{1,0:T(8,128)S(1)} %collective-permute-done.10.refs_3_), channel_id=1, source_target_pairs={{0,24},{1,7},{2,26},{3,1},{4,28},{5,3},{6,30},{7,5},{8,0},{9,15},{... | collective-permute-start | bytes 1277960 | tf_op jit(solution)/shard_map/ppermute | solution.py:54
  59.1 1.9 %collective-permute-start.15 = (f32[416,256]{1,0:T(8,128)}, f32[416,256]{1,0:T(8,128)}, u32[]{:S(2)}, u32[]{:S(2)}) collective-permute-start(f32[416,256]{1,0:T(8,128)} %copy-done.3), channel_id=1, source_target_pairs={{0,1},{1,0},{2,3},{3,2},{4,5},{5,4},{6,7},{7,6},{8,9},{9,8},{10,11... | collective-permute-start | bytes 1277960 | tf_op jit(solution)/shard_map/ppermute | solution.py:58
  61.1 10.0 %collective-permute-done.14.refs_7_ = f32[416,256]{1,0:T(8,128)} collective-permute-done((f32[416,256]{1,0:T(8,128)}, f32[416,256]{1,0:T(8,128)}, u32[]{:S(2)}, u32[]{:S(2)}) %collective-permute-start.14) | collective-permute-done | bytes 426016 | tf_op jit(solution)/shard_map/ppermute | solution.py:54
  71.1 1.1 collective-permute-start.6
  72.3 0.7 collective-permute-start.19
  73.0 2.7 %collective-permute-done.11.refs_5_ = f32[416,256]{1,0:T(8,128)} collective-permute-done((f32[416,256]{1,0:T(8,128)S(1)}, f32[416,256]{1,0:T(8,128)}, u32[]{:S(2)}, u32[]{:S(2)}) %collective-permute-start.11) | collective-permute-done | bytes 426016 | tf_op jit(solution)/shard_map/ppermute | solution.py:54
  75.7 2.4 %collective-permute-start.3 = (f32[416,256]{1,0:T(8,128)}, f32[416,256]{1,0:T(8,128)}, u32[]{:S(2)}, u32[]{:S(2)}) collective-permute-start(f32[416,256]{1,0:T(8,128)} %collective-permute-done.2.refs_4_), channel_id=1, source_target_pairs={{0,6},{1,25},{2,0},{3,27},{4,2},{5,29},{6,4},{7,31},{8,14},{9,1},{... | collective-permute-start | bytes 1277960 | tf_op jit(solution)/shard_map/ppermute | solution.py:54
  78.8 0.7 collective-permute-start.16
  79.8 1.0 copy-done.2
  80.8 1.0 copy-done.6
  81.8 4.3 %shard_map.86 = (f32[416,256]{1,0:T(8,128)S(1)}, f32[416,256]{1,0:T(8,128)S(1)}) custom-call(s32[3]{0:T(128)S(1)} %pad_add_fusion.refs_0_.where_ref, s32[1]{0:T(128)} %bitcast.13.refs_1_, f32[416,13312]{1,0:T(8,128)} %bitcast.21, f32[416,256]{1,0:T(8,128)S(1)} %collective-permute-done.28.refs_3_, f32[416,256]{1,0:T(8,128)S(1)} %collective-permute-done.4.refs_4_, ...), custom_call_target="tpu_custom_call" | custom-call | flops 1635778560 | bytes 6389760 | tf_op jit(solution)/shard_map/pallas_call | solution.py:261
  86.2 0.7 copy-done.11
  86.9 0.8 copy-done.14
  87.7 1.5 %shard_map.91 = (f32[416,256]{1,0:T(8,128)S(1)}, f32[416,256]{1,0:T(8,128)S(1)}) custom-call(s32[3]{0:T(128)S(1)} %pad_add_fusion.refs_0_.where_ref, f32[16,56,256]{2,1,0:T(8,128)S(1)} %all-to-all-done.in_ref), custom_call_target="tpu_custom_call" | custom-call | flops 400000000 | bytes 2000000 | tf_op jit(solution)/shard_map/pallas_call | solution.py:153
  89.2 1.0 copy-done.8
  90.2 1.0 copy-done.10
  91.3 1.0 copy-done.12
  92.3 5.3 %shard_map.87.refs_9_ = f32[416,256]{1,0:T(8,128)S(1)} custom-call(s32[3]{0:T(128)S(1)} %pad_add_fusion.refs_0_.where_ref, s32[1]{0:T(128)} %bitcast.14.refs_1_, f32[416,13312]{1,0:T(8,128)} %bitcast.22, f32[416,256]{1,0:T(8,128)S(1)} %collective-permute-done.12.refs_3_, f32[416,256]{1,0:T(8,128)S(1)} %collective-permute-done.24.refs_4_, ...), custom_call_target="tpu_custom_call" | custom-call | flops 1962934272 | bytes 7667712 | tf_op jit(solution)/shard_map/pallas_call | solution.py:261
  98.4 5.6 %shard_map.88.refs_13_ = f32[416,256]{1,0:T(8,128)S(1)} custom-call(s32[3]{0:T(128)S(1)} %pad_add_fusion.refs_0_.where_ref, s32[1]{0:T(128)} %bitcast.15.refs_1_, f32[416,13312]{1,0:T(8,128)} %bitcast.23, f32[416,256]{1,0:T(8,128)S(1)} %collective-permute-done.10.refs_3_, f32[416,256]{1,0:T(8,128)} %collective-permute-done.1.refs_4_, ...), custom_call_target="tpu_custom_call" | custom-call | flops 1962934272 | bytes 7667712 | tf_op jit(solution)/shard_map/pallas_call | solution.py:261
  104.1 8.0 %shard_map.89.refs_7_ = f32[416,256]{1,0:T(8,128)S(1)} custom-call(s32[3]{0:T(128)S(1)} %pad_add_fusion.refs_0_.where_ref, s32[1]{0:T(128)} %bitcast.16.refs_1_, f32[416,13312]{1,0:T(8,128)} %bitcast.24, f32[416,256]{1,0:T(8,128)S(1)} %copy-done.4, f32[416,256]{1,0:T(8,128)} %collective-permute-done.2.refs_4_, f32[416,256]{1,0:T(8,128)} %collective-permute-done.11.refs_5_, ...), custom_call_target="tpu_custom_call" | custom-call | flops 3271557120 | bytes 12779520 | tf_op jit(solution)/shard_map/pallas_call | solution.py:261
  112.2 4.8 %shard_map.92 = (f32[416,256]{1,0:T(8,128)S(1)}, f32[128,256]{1,0:T(8,128)S(1)}) custom-call(s32[3]{0:T(128)S(1)} %pad_add_fusion.refs_0_.where_ref, s32[1]{0:T(128)} %bitcast.17.refs_1_, f32[416,13312]{1,0:T(8,128)} %bitcast.25, f32[416,256]{1,0:T(8,128)} %collective-permute-done.3.refs_3_, f32[416,256]{1,0:T(8,128)} %collective-permute-done.6.refs_4_, ...), custom_call_target="tpu_custom_call" | custom-call | flops 1308622848 | bytes 5111808 | tf_op jit(solution)/shard_map/pallas_call | solution.py:261
  117.5 1.1 collective-permute-done.34.sibling_ref
  118.6 8.4 %shard_map.93 = (f32[416,128]{1,0:T(8,128)}, f32[128,128]{1,0:T(8,128)}) custom-call(s32[3]{0:T(128)S(1)} %pad_add_fusion.refs_0_.where_ref, s32[1]{0:T(128)} %bitcast.18.rank_ref, f32[416,256]{1,0:T(8,128)S(1)} %get-tuple-element.13.sum_ref, f32[416,256]{1,0:T(8,128)S(1)} %copy-done.15, f32[128,256]{1,0:T(8,128)S(1)} %get-tuple-element.15.up_ref, ...), custom_call_target="tpu_custom_call" | custom-call | flops 2000000000 | bytes 2000000 | tf_op jit(solution)/shard_map/pallas_call | solution.py:409
  (66 shorter events, 3.2 us)
Async XLA Ops:
  0.6 116.9 %copy-start = (s32[1,16,128]{2,1,0:T(8,128)S(1)}, s32[1,16,128]{2,1,0:T(8,128)}, u32[]{:S(2)}) copy-start(s32[1,16,128]{2,1,0:T(8,128)} %param.13) | copy-start | bytes 24580
  0.6 19.7 %collective-permute-start.4 = (f32[416,256]{1,0:T(8,128)}, f32[416,256]{1,0:T(8,128)S(1)}, u32[]{:S(2)}, u32[]{:S(2)}) collective-permute-start(f32[416,256]{1,0:T(8,128)} %bitcast.26), channel_id=1, source_target_pairs={{0,2},{1,9},{2,4},{3,11},{4,6},{5,13},{6,0},{7,15},{8,10},{9,17},{... | collective-permute-start | bytes 1277960 | tf_op jit(solution)/shard_map/ppermute | solution.py:54
  3.2 18.5 %collective-permute-start = (f32[416,256]{1,0:T(8,128)}, f32[416,256]{1,0:T(8,128)S(1)}, u32[]{:S(2)}, u32[]{:S(2)}) collective-permute-start(f32[416,256]{1,0:T(8,128)} %bitcast.27), channel_id=1, source_target_pairs={{0,6},{1,25},{2,0},{3,27},{4,2},{5,29},{6,4},{7,31},{8,14},{9,1},{... | collective-permute-start | bytes 1277960 | tf_op jit(solution)/shard_map/ppermute | solution.py:54
  5.4 12.9 %collective-permute-start.31 = (f32[384,256]{1,0:T(8,128)}, f32[384,256]{1,0:T(8,128)S(1)}, u32[]{:S(2)}, u32[]{:S(2)}) collective-permute-start(f32[384,256]{1,0:T(8,128)} %bitcast.31), channel_id=1, source_target_pairs={{0,32},{32,64},{64,96},{96,0},{1,33},{33,65},{65,97},{97,1},{2,34}... | collective-permute-start | bytes 1179656 | tf_op jit(solution)/shard_map/ppermute | solution.py:437
  6.7 11.0 %collective-permute-start.32 = (s32[1,384]{1,0:T(1,128)}, s32[1,384]{1,0:T(1,128)S(1)}, u32[]{:S(2)}, u32[]{:S(2)}) collective-permute-start(s32[1,384]{1,0:T(1,128)} %param.10), channel_id=1, source_target_pairs={{0,32},{32,64},{64,96},{96,0},{1,33},{33,65},{65,97},{97,1},{2,34}... | collective-permute-start | bytes 4616 | tf_op jit(solution)/shard_map/ppermute | solution.py:438
  8.0 13.8 %collective-permute-start.28 = (f32[416,256]{1,0:T(8,128)}, f32[416,256]{1,0:T(8,128)S(1)}, u32[]{:S(2)}, u32[]{:S(2)}) collective-permute-start(f32[416,256]{1,0:T(8,128)} %bitcast.28), channel_id=1, source_target_pairs={{0,1},{1,0},{2,3},{3,2},{4,5},{5,4},{6,7},{7,6},{8,9},{9,8},{10,11... | collective-permute-start | bytes 1277960 | tf_op jit(solution)/shard_map/ppermute | solution.py:58
  17.7 8.7 %collective-permute-start.12 = (f32[416,256]{1,0:T(8,128)}, f32[416,256]{1,0:T(8,128)S(1)}, u32[]{:S(2)}, u32[]{:S(2)}) collective-permute-start(f32[416,256]{1,0:T(8,128)} %bitcast.29), channel_id=1, source_target_pairs={{0,8},{1,3},{2,10},{3,5},{4,12},{5,7},{6,14},{7,1},{8,16},{9,11},{... | collective-permute-start | bytes 1277960 | tf_op jit(solution)/shard_map/ppermute | solution.py:54
  18.2 11.7 %collective-permute-start.24 = (f32[416,256]{1,0:T(8,128)}, f32[416,256]{1,0:T(8,128)S(1)}, u32[]{:S(2)}, u32[]{:S(2)}) collective-permute-start(f32[416,256]{1,0:T(8,128)} %bitcast.30), channel_id=1, source_target_pairs={{0,24},{1,7},{2,26},{3,1},{4,28},{5,3},{6,30},{7,5},{8,0},{9,15},{... | collective-permute-start | bytes 1277960 | tf_op jit(solution)/shard_map/ppermute | solution.py:54
  20.3 9.6 %collective-permute-start.29 = (f32[416,256]{1,0:T(8,128)S(1)}, f32[416,256]{1,0:T(8,128)S(1)}, u32[]{:S(2)}, u32[]{:S(2)}) collective-permute-start(f32[416,256]{1,0:T(8,128)S(1)} %collective-permute-done.4.refs_4_), channel_id=1, source_target_pairs={{0,1},{1,0},{2,3},{3,2},{4,5},{5,4},{6,7},{7,6},{8,9},{9,8},{10,11... | collective-permute-start | bytes 1277960 | tf_op jit(solution)/shard_map/ppermute | solution.py:58
  21.7 9.3 %collective-permute-start.30 = (f32[416,256]{1,0:T(8,128)S(1)}, f32[416,256]{1,0:T(8,128)S(1)}, u32[]{:S(2)}, u32[]{:S(2)}) collective-permute-start(f32[416,256]{1,0:T(8,128)S(1)} %collective-permute-done.refs_5_), channel_id=1, source_target_pairs={{0,1},{1,0},{2,3},{3,2},{4,5},{5,4},{6,7},{7,6},{8,9},{9,8},{10,11... | collective-permute-start | bytes 1277960 | tf_op jit(solution)/shard_map/ppermute | solution.py:58
  21.8 10.4 %collective-permute-start.5 = (f32[416,256]{1,0:T(8,128)S(1)}, f32[416,256]{1,0:T(8,128)}, u32[]{:S(2)}, u32[]{:S(2)}) collective-permute-start(f32[416,256]{1,0:T(8,128)S(1)} %collective-permute-done.4.refs_4_), channel_id=1, source_target_pairs={{0,2},{1,9},{2,4},{3,11},{4,6},{5,13},{6,0},{7,15},{8,10},{9,17},{... | collective-permute-start | bytes 1277960 | tf_op jit(solution)/shard_map/ppermute | solution.py:54
  26.4 5.9 %collective-permute-start.25 = (f32[416,256]{1,0:T(8,128)S(1)}, f32[416,256]{1,0:T(8,128)S(1)}, u32[]{:S(2)}, u32[]{:S(2)}) collective-permute-start(f32[416,256]{1,0:T(8,128)S(1)} %collective-permute-done.12.refs_3_), channel_id=1, source_target_pairs={{0,1},{1,0},{2,3},{3,2},{4,5},{5,4},{6,7},{7,6},{8,9},{9,8},{10,11... | collective-permute-start | bytes 1277960 | tf_op jit(solution)/shard_map/ppermute | solution.py:58
  29.9 5.8 %collective-permute-start.26 = (f32[416,256]{1,0:T(8,128)S(1)}, f32[416,256]{1,0:T(8,128)S(1)}, u32[]{:S(2)}, u32[]{:S(2)}) collective-permute-start(f32[416,256]{1,0:T(8,128)S(1)} %collective-permute-done.24.refs_4_), channel_id=1, source_target_pairs={{0,1},{1,0},{2,3},{3,2},{4,5},{5,4},{6,7},{7,6},{8,9},{9,8},{10,11... | collective-permute-start | bytes 1277960 | tf_op jit(solution)/shard_map/ppermute | solution.py:58
  29.9 19.7 %copy-start.1 = (f32[416,256]{1,0:T(8,128)}, f32[416,256]{1,0:T(8,128)S(1)}, u32[]{:S(2)}) copy-start(f32[416,256]{1,0:T(8,128)S(1)} %collective-permute-done.29.refs_6_) | copy-start | bytes 1277956
  29.9 7.4 %collective-permute-start.10 = (f32[416,256]{1,0:T(8,128)S(1)}, f32[416,256]{1,0:T(8,128)S(1)}, u32[]{:S(2)}, u32[]{:S(2)}) collective-permute-start(f32[416,256]{1,0:T(8,128)S(1)} %collective-permute-done.4.refs_4_), channel_id=1, source_target_pairs={{0,24},{1,7},{2,26},{3,1},{4,28},{5,3},{6,30},{7,5},{8,0},{9,15},{... | collective-permute-start | bytes 1277960 | tf_op jit(solution)/shard_map/ppermute | solution.py:54
  31.7 8.6 %collective-permute-start.1 = (f32[416,256]{1,0:T(8,128)S(1)}, f32[416,256]{1,0:T(8,128)}, u32[]{:S(2)}, u32[]{:S(2)}) collective-permute-start(f32[416,256]{1,0:T(8,128)S(1)} %collective-permute-done.refs_5_), channel_id=1, source_target_pairs={{0,8},{1,3},{2,10},{3,5},{4,12},{5,7},{6,14},{7,1},{8,16},{9,11},{... | collective-permute-start | bytes 1277960 | tf_op jit(solution)/shard_map/ppermute | solution.py:54
  32.2 12.7 %collective-permute-start.20 = (f32[416,256]{1,0:T(8,128)S(1)}, f32[416,256]{1,0:T(8,128)}, u32[]{:S(2)}, u32[]{:S(2)}) collective-permute-start(f32[416,256]{1,0:T(8,128)S(1)} %collective-permute-done.4.refs_4_), channel_id=1, source_target_pairs={{0,8},{1,3},{2,10},{3,5},{4,12},{5,7},{6,14},{7,1},{8,16},{9,11},{... | collective-permute-start | bytes 1277960 | tf_op jit(solution)/shard_map/ppermute | solution.py:54
  32.2 0.8 copy-start.7
  33.0 13.8 %collective-permute-start.9 = (f32[416,256]{1,0:T(8,128)S(1)}, f32[416,256]{1,0:T(8,128)S(1)}, u32[]{:S(2)}, u32[]{:S(2)}) collective-permute-start(f32[416,256]{1,0:T(8,128)S(1)} %collective-permute-done.refs_5_), channel_id=1, source_target_pairs={{0,24},{1,7},{2,26},{3,1},{4,28},{5,3},{6,30},{7,5},{8,0},{9,15},{... | collective-permute-start | bytes 1277960 | tf_op jit(solution)/shard_map/ppermute | solution.py:54
  35.7 0.8 copy-start.9
  36.5 17.3 %collective-permute-start.13 = (f32[416,256]{1,0:T(8,128)S(1)}, f32[416,256]{1,0:T(8,128)}, u32[]{:S(2)}, u32[]{:S(2)}) collective-permute-start(f32[416,256]{1,0:T(8,128)S(1)} %collective-permute-done.12.refs_3_), channel_id=1, source_target_pairs={{0,8},{1,3},{2,10},{3,5},{4,12},{5,7},{6,14},{7,1},{8,16},{9,11},{... | collective-permute-start | bytes 1277960 | tf_op jit(solution)/shard_map/ppermute | solution.py:54
  37.4 19.1 %collective-permute-start.27 = (f32[416,256]{1,0:T(8,128)}, f32[416,256]{1,0:T(8,128)}, u32[]{:S(2)}, u32[]{:S(2)}) collective-permute-start(f32[416,256]{1,0:T(8,128)} %collective-permute-done.5.refs_5_), channel_id=1, source_target_pairs={{0,1},{1,0},{2,3},{3,2},{4,5},{5,4},{6,7},{7,6},{8,9},{9,8},{10,11... | collective-permute-start | bytes 1277960 | tf_op jit(solution)/shard_map/ppermute | solution.py:58
  40.3 16.1 %collective-permute-start.21 = (f32[416,256]{1,0:T(8,128)S(1)}, f32[416,256]{1,0:T(8,128)}, u32[]{:S(2)}, u32[]{:S(2)}) collective-permute-start(f32[416,256]{1,0:T(8,128)S(1)} %collective-permute-done.10.refs_3_), channel_id=1, source_target_pairs={{0,1},{1,0},{2,3},{3,2},{4,5},{5,4},{6,7},{7,6},{8,9},{9,8},{10,11... | collective-permute-start | bytes 1277960 | tf_op jit(solution)/shard_map/ppermute | solution.py:58
  44.9 14.2 %collective-permute-start.22 = (f32[416,256]{1,0:T(8,128)}, f32[416,256]{1,0:T(8,128)}, u32[]{:S(2)}, u32[]{:S(2)}) collective-permute-start(f32[416,256]{1,0:T(8,128)} %collective-permute-done.1.refs_4_), channel_id=1, source_target_pairs={{0,1},{1,0},{2,3},{3,2},{4,5},{5,4},{6,7},{7,6},{8,9},{9,8},{10,11... | collective-permute-start | bytes 1277960 | tf_op jit(solution)/shard_map/ppermute | solution.py:58
  47.6 13.4 %collective-permute-start.23 = (f32[416,256]{1,0:T(8,128)}, f32[416,256]{1,0:T(8,128)}, u32[]{:S(2)}, u32[]{:S(2)}) collective-permute-start(f32[416,256]{1,0:T(8,128)} %collective-permute-done.20.refs_5_), channel_id=1, source_target_pairs={{0,1},{1,0},{2,3},{3,2},{4,5},{5,4},{6,7},{7,6},{8,9},{9,8},{10,11... | collective-permute-start | bytes 1277960 | tf_op jit(solution)/shard_map/ppermute | solution.py:58
  49.6 38.1 %all-to-all-start = ((f32[16,56,256]{2,1,0:T(8,128)}), f32[16,56,256]{2,1,0:T(8,128)S(1)}, u32[]{:S(2)}, u32[]{:S(2)}) async-start(f32[16,56,256]{2,1,0:T(8,128)} %bitcast.7), calls=%async_computation | async-start | bytes 1835008 | tf_op jit(solution)/shard_map/all_to_all | solution.py:440
  53.8 17.3 %collective-permute-start.14 = (f32[416,256]{1,0:T(8,128)}, f32[416,256]{1,0:T(8,128)}, u32[]{:S(2)}, u32[]{:S(2)}) collective-permute-start(f32[416,256]{1,0:T(8,128)} %collective-permute-done.5.refs_5_), channel_id=1, source_target_pairs={{0,24},{1,7},{2,26},{3,1},{4,28},{5,3},{6,30},{7,5},{8,0},{9,15},{... | collective-permute-start | bytes 1277960 | tf_op jit(solution)/shard_map/ppermute | solution.py:54
  56.4 15.9 %collective-permute-start.2 = (f32[416,256]{1,0:T(8,128)}, f32[416,256]{1,0:T(8,128)}, u32[]{:S(2)}, u32[]{:S(2)}) collective-permute-start(f32[416,256]{1,0:T(8,128)} %collective-permute-done.1.refs_4_), channel_id=1, source_target_pairs={{0,8},{1,3},{2,10},{3,5},{4,12},{5,7},{6,14},{7,1},{8,16},{9,11},{... | collective-permute-start | bytes 1277960 | tf_op jit(solution)/shard_map/ppermute | solution.py:54
  56.4 19.2 %collective-permute-start.11 = (f32[416,256]{1,0:T(8,128)S(1)}, f32[416,256]{1,0:T(8,128)}, u32[]{:S(2)}, u32[]{:S(2)}) collective-permute-start(f32[416,256]{1,0:T(8,128)S(1)} %collective-permute-done.10.refs_3_), channel_id=1, source_target_pairs={{0,24},{1,7},{2,26},{3,1},{4,28},{5,3},{6,30},{7,5},{8,0},{9,15},{... | collective-permute-start | bytes 1277960 | tf_op jit(solution)/shard_map/ppermute | solution.py:54
  59.1 19.7 %collective-permute-start.15 = (f32[416,256]{1,0:T(8,128)}, f32[416,256]{1,0:T(8,128)}, u32[]{:S(2)}, u32[]{:S(2)}) collective-permute-start(f32[416,256]{1,0:T(8,128)} %copy-done.3), channel_id=1, source_target_pairs={{0,1},{1,0},{2,3},{3,2},{4,5},{5,4},{6,7},{7,6},{8,9},{9,8},{10,11... | collective-permute-start | bytes 1277960 | tf_op jit(solution)/shard_map/ppermute | solution.py:58
  61.0 18.5 %collective-permute-start.18 = (f32[416,256]{1,0:T(8,128)}, f32[416,256]{1,0:T(8,128)}, u32[]{:S(2)}, u32[]{:S(2)}) collective-permute-start(f32[416,256]{1,0:T(8,128)} %collective-permute-done.13.refs_6_), channel_id=1, source_target_pairs={{0,1},{1,0},{2,3},{3,2},{4,5},{5,4},{6,7},{7,6},{8,9},{9,8},{10,11... | collective-permute-start | bytes 1277960 | tf_op jit(solution)/shard_map/ppermute | solution.py:58
  71.1 26.5 %collective-permute-start.6 = (f32[416,256]{1,0:T(8,128)}, f32[416,256]{1,0:T(8,128)}, u32[]{:S(2)}, u32[]{:S(2)}) collective-permute-start(f32[416,256]{1,0:T(8,128)} %collective-permute-done.5.refs_5_), channel_id=1, source_target_pairs={{0,8},{1,3},{2,10},{3,5},{4,12},{5,7},{6,14},{7,1},{8,16},{9,11},{... | collective-permute-start | bytes 1277960 | tf_op jit(solution)/shard_map/ppermute | solution.py:54
  72.3 25.6 %collective-permute-start.19 = (f32[416,256]{1,0:T(8,128)}, f32[416,256]{1,0:T(8,128)}, u32[]{:S(2)}, u32[]{:S(2)}) collective-permute-start(f32[416,256]{1,0:T(8,128)} %collective-permute-done.14.refs_7_), channel_id=1, source_target_pairs={{0,1},{1,0},{2,3},{3,2},{4,5},{5,4},{6,7},{7,6},{8,9},{9,8},{10,11... | collective-permute-start | bytes 1277960 | tf_op jit(solution)/shard_map/ppermute | solution.py:58
  75.7 22.5 %collective-permute-start.3 = (f32[416,256]{1,0:T(8,128)}, f32[416,256]{1,0:T(8,128)}, u32[]{:S(2)}, u32[]{:S(2)}) collective-permute-start(f32[416,256]{1,0:T(8,128)} %collective-permute-done.2.refs_4_), channel_id=1, source_target_pairs={{0,6},{1,25},{2,0},{3,27},{4,2},{5,29},{6,4},{7,31},{8,14},{9,1},{... | collective-permute-start | bytes 1277960 | tf_op jit(solution)/shard_map/ppermute | solution.py:54
  78.8 25.2 %collective-permute-start.16 = (f32[416,256]{1,0:T(8,128)}, f32[416,256]{1,0:T(8,128)}, u32[]{:S(2)}, u32[]{:S(2)}) collective-permute-start(f32[416,256]{1,0:T(8,128)} %collective-permute-done.2.refs_4_), channel_id=1, source_target_pairs={{0,1},{1,0},{2,3},{3,2},{4,5},{5,4},{6,7},{7,6},{8,9},{9,8},{10,11... | collective-permute-start | bytes 1277960 | tf_op jit(solution)/shard_map/ppermute | solution.py:58
  79.5 24.5 %collective-permute-start.17 = (f32[416,256]{1,0:T(8,128)}, f32[416,256]{1,0:T(8,128)}, u32[]{:S(2)}, u32[]{:S(2)}) collective-permute-start(f32[416,256]{1,0:T(8,128)} %collective-permute-done.11.refs_5_), channel_id=1, source_target_pairs={{0,1},{1,0},{2,3},{3,2},{4,5},{5,4},{6,7},{7,6},{8,9},{9,8},{10,11... | collective-permute-start | bytes 1277960 | tf_op jit(solution)/shard_map/ppermute | solution.py:58
  79.8 1.0 copy-start.2
  80.8 1.0 copy-start.6
  89.2 1.0 copy-start.8
  90.2 1.0 copy-start.10
  91.3 1.0 copy-start.12
  92.3 11.8 %copy-start.4 = (f32[416,256]{1,0:T(8,128)S(1)}, f32[416,256]{1,0:T(8,128)}, u32[]{:S(2)}) copy-start(f32[416,256]{1,0:T(8,128)} %copy-done.3) | copy-start | bytes 1277956
  97.6 14.5 %collective-permute-start.33 = (f32[416,256]{1,0:T(8,128)S(1)}, f32[416,256]{1,0:T(8,128)S(1)}, u32[]{:S(2)}, u32[]{:S(2)}) collective-permute-start(f32[416,256]{1,0:T(8,128)S(1)} %get-tuple-element.12), channel_id=1, source_target_pairs={{0,1},{1,0},{2,3},{3,2},{4,5},{5,4},{6,7},{7,6},{8,9},{9,8},{10,11... | collective-permute-start | bytes 1277960 | tf_op jit(solution)/shard_map/ppermute | solution.py:58
  97.9 14.2 %collective-permute-start.8 = (f32[416,256]{1,0:T(8,128)}, f32[416,256]{1,0:T(8,128)S(1)}, u32[]{:S(2)}, u32[]{:S(2)}) collective-permute-start(f32[416,256]{1,0:T(8,128)} %collective-permute-done.6.refs_4_), channel_id=1, source_target_pairs={{0,1},{1,0},{2,3},{3,2},{4,5},{5,4},{6,7},{7,6},{8,9},{9,8},{10,11... | collective-permute-start | bytes 1277960 | tf_op jit(solution)/shard_map/ppermute | solution.py:58
  98.2 13.9 %collective-permute-start.7 = (f32[416,256]{1,0:T(8,128)}, f32[416,256]{1,0:T(8,128)S(1)}, u32[]{:S(2)}, u32[]{:S(2)}) collective-permute-start(f32[416,256]{1,0:T(8,128)} %collective-permute-done.3.refs_3_), channel_id=1, source_target_pairs={{0,1},{1,0},{2,3},{3,2},{4,5},{5,4},{6,7},{7,6},{8,9},{9,8},{10,11... | collective-permute-start | bytes 1277960 | tf_op jit(solution)/shard_map/ppermute | solution.py:58
  98.4 13.7 %copy-start.13 = (s32[1,1,128]{2,1,0:T(1,128)S(1)}, s32[1,1,128]{2,1,0:T(1,128)}, u32[]{:S(2)}) copy-start(s32[1,1,128]{2,1,0:T(1,128)} %param.11) | copy-start | bytes 1540
  104.1 14.5 %copy-start.15 = (f32[416,256]{1,0:T(8,128)S(1)}, f32[416,256]{1,0:T(8,128)}, u32[]{:S(2)}) copy-start(f32[416,256]{1,0:T(8,128)} %copy-done.14) | copy-start | bytes 1277956
  116.9 1.6 %collective-permute-start.34 = (f32[128,256]{1,0:T(8,128)S(1)}, f32[128,256]{1,0:T(8,128)S(1)}, u32[]{:S(2)}, u32[]{:S(2)}) collective-permute-start(f32[128,256]{1,0:T(8,128)S(1)} %get-tuple-element.15.up_ref), channel_id=1, source_target_pairs={{0,1},{1,0},{2,3},{3,2},{4,5},{5,4},{6,7},{7,6},{8,9},{9,8},{10,11... | collective-permute-start | bytes 393224 | tf_op jit(solution)/shard_map/ppermute | solution.py:58
  (4 other events, 3.0 us)

commit v3 on v2

--- a/solution.py
+++ b/solution.py
@@ -321,39 +321,44 @@
     return values[0]
 
 
-def eliminate(panel, at, first):
+def eliminate(panels, at, first):
     lane = lax.broadcasted_iota(jnp.int32, (8, RANK), 1)
     sub = lax.broadcasted_iota(jnp.int32, (8, RANK), 0)
     inside = (lane >= first) & (lane < first + 8)
-    tile = panel[at]
-    rows = [jnp.broadcast_to(tile[a : a + 1, :], (8, RANK)) for a in range(8)]
+    upper = sub < 4
+    tiles = [panel[at] for panel in panels]
+    rows = [jnp.where(upper, *(jnp.broadcast_to(t[a : a + 1, :], (8, RANK)) for t in tiles)) for a in range(8)]
     s = [[None] * 8 for _ in range(8)]
     for a in range(8):
         for b in range(a, 8):
             s[a][b] = s[b][a] = jnp.broadcast_to(rows[a][:, first + b : first + b + 1], (8, RANK))
     d = small_inverse(s)
-    scaled = []
+    both = []
     for a in range(8):
         own = by_position(lane, d[a])
-        scaled.append(jnp.where(inside, own, total_of([d[a][b] * rows[b] for b in range(8)])))
-    out = []
-    for t, old in enumerate(panel):
-        if t == at:
-            out.append(by_position(sub, scaled))
-            continue
-        columns = [jnp.broadcast_to(old[:, first + a : first + a + 1], (8, RANK)) for a in range(8)]
-        out.append(jnp.where(inside, 0.0, old) - total_of([c * r for c, r in zip(columns, scaled)]))
-    return out
-
-
-def invert(refs, tiles=8):
+        both.append(jnp.where(inside, own, total_of([d[a][b] * rows[b] for b in range(8)])))
+    results = []
+    for panel, half in zip(panels, (0, 4)):
+        scaled = [jnp.broadcast_to(v[half : half + 1, :], (8, RANK)) for v in both]
+        out = []
+        for t, old in enumerate(panel):
+            if t == at:
+                out.append(by_position(sub, scaled))
+                continue
+            columns = [jnp.broadcast_to(old[:, first + a : first + a + 1], (8, RANK)) for a in range(8)]
+            out.append(jnp.where(inside, 0.0, old) - total_of([c * r for c, r in zip(columns, scaled)]))
+        results.append(out)
+    return results
+
+
+def invert(refs, tiles=4):
     lane = lax.broadcasted_iota(jnp.int32, (RANK, RANK), 1)
     row = lax.broadcasted_iota(jnp.int32, (RANK, RANK), 0)
     height = 8 * tiles
     for start in range(0, RANK, height):
         panels = [[ref[start + 8 * t : start + 8 * t + 8, :] for t in range(tiles)] for ref in refs]
         for t in range(tiles):
-            panels = [eliminate(panel, t, start + 8 * t) for panel in panels]
+            panels = eliminate(panels, t, start + 8 * t)
         for ref, panel in zip(refs, panels):
             old = ref[...]
             inside = (lane >= start) & (lane < start + height)

time: 127 us -> 126 us (level)
  no operation moved by 1% of the time
where the time goes in v3:
time: 126 us
  starting transfers between devices  43.1 us (34%)
  Pallas kernels  38.8 us (31%)
  waiting for transfers between devices  32.7 us (26%)
  local copies, waits for them, and re-layouts  9.66 us (8%)
  between operations  1.51 us (1%)
    pallas_call x5, Pallas kernels, product(): pl.pallas_call(kernel, out_shape=tuple(out_shape), in_specs=specs, out_sp...  28 us
    ppermute x15, waiting for transfers between devices, chips_step(): return lax.ppermute(value, BLK, pairs)  22.5 us
    ppermute x15, starting transfers between devices, chips_step(): return lax.ppermute(value, BLK, pairs)  20.5 us
    ppermute x18, starting transfers between devices, swap_cores(): return lax.ppermute(value, 'blk_2', [(0, 1), (1, 0)])  15.8 us
    unnamed x32, local copies, waits for them, and re-layouts  9.66 us
    ppermute x1, waiting for transfers between devices, body(): dest = lax.ppermute(child_dest, 'front', ahead)  9.06 us
    pallas_call x1, Pallas kernels, finish(): pl.pallas_call(finish_kernel, out_shape=(jax.ShapeDtypeStruct((HEIGHT, RA...  7.25 us
    all_to_all x1, starting transfers between devices, body(): arrived = lax.all_to_all(sending, ('blk_0', 'blk_1'), 0, 0, tiled=True)  4.12 us
  transfers between devices with their start and end apart: 36, of which 8 were waited for; matrix products, arithmetic and copies ran while one was open for 0% of the time, Pallas kernels for 21%

profile of v3, /device:TPU:1, one launch (start us, length us, event | category | flops | bytes accessed | tf_op | source)
XLA Modules:
  0.0 125.8 jit_solution(15617584833724881178)
XLA Ops:
  0.6 2.5 %collective-permute-start.4 = (f32[416,256]{1,0:T(8,128)}, f32[416,256]{1,0:T(8,128)S(1)}, u32[]{:S(2)}, u32[]{:S(2)}) collective-permute-start(f32[416,256]{1,0:T(8,128)} %bitcast.26), channel_id=1, source_target_pairs={{0,2},{1,9},{2,4},{3,11},{4,6},{5,13},{6,0},{7,15},{8,10},{9,17},{... | collective-permute-start | bytes 1277960 | tf_op jit(solution)/shard_map/ppermute | solution.py:54
  3.2 2.2 %collective-permute-start = (f32[416,256]{1,0:T(8,128)}, f32[416,256]{1,0:T(8,128)S(1)}, u32[]{:S(2)}, u32[]{:S(2)}) collective-permute-start(f32[416,256]{1,0:T(8,128)} %bitcast.27), channel_id=1, source_target_pairs={{0,6},{1,25},{2,0},{3,27},{4,2},{5,29},{6,4},{7,31},{8,14},{9,1},{... | collective-permute-start | bytes 1277960 | tf_op jit(solution)/shard_map/ppermute | solution.py:54
  5.4 1.3 %collective-permute-start.31 = (f32[384,256]{1,0:T(8,128)}, f32[384,256]{1,0:T(8,128)S(1)}, u32[]{:S(2)}, u32[]{:S(2)}) collective-permute-start(f32[384,256]{1,0:T(8,128)} %bitcast.31), channel_id=1, source_target_pairs={{0,32},{32,64},{64,96},{96,0},{1,33},{33,65},{65,97},{97,1},{2,34}... | collective-permute-start | bytes 1179656 | tf_op jit(solution)/shard_map/ppermute | solution.py:442
  6.7 1.3 %collective-permute-start.32 = (s32[1,384]{1,0:T(1,128)}, s32[1,384]{1,0:T(1,128)S(1)}, u32[]{:S(2)}, u32[]{:S(2)}) collective-permute-start(s32[1,384]{1,0:T(1,128)} %param.10), channel_id=1, source_target_pairs={{0,32},{32,64},{64,96},{96,0},{1,33},{33,65},{65,97},{97,1},{2,34}... | collective-permute-start | bytes 4616 | tf_op jit(solution)/shard_map/ppermute | solution.py:443
  8.0 0.6 collective-permute-start.28
  8.6 9.1 %collective-permute-done.32.dest_ref = s32[1,384]{1,0:T(1,128)S(1)} collective-permute-done((s32[1,384]{1,0:T(1,128)}, s32[1,384]{1,0:T(1,128)S(1)}, u32[]{:S(2)}, u32[]{:S(2)}) %collective-permute-start.32) | collective-permute-done | bytes 1568 | tf_op jit(solution)/shard_map/ppermute | solution.py:443
  18.2 2.1 %collective-permute-start.24 = (f32[416,256]{1,0:T(8,128)}, f32[416,256]{1,0:T(8,128)S(1)}, u32[]{:S(2)}, u32[]{:S(2)}) collective-permute-start(f32[416,256]{1,0:T(8,128)} %bitcast.30), channel_id=1, source_target_pairs={{0,24},{1,7},{2,26},{3,1},{4,28},{5,3},{6,30},{7,5},{8,0},{9,15},{... | collective-permute-start | bytes 1277960 | tf_op jit(solution)/shard_map/ppermute | solution.py:54
  20.3 1.3 %collective-permute-start.29 = (f32[416,256]{1,0:T(8,128)S(1)}, f32[416,256]{1,0:T(8,128)S(1)}, u32[]{:S(2)}, u32[]{:S(2)}) collective-permute-start(f32[416,256]{1,0:T(8,128)S(1)} %collective-permute-done.4.refs_4_), channel_id=1, source_target_pairs={{0,1},{1,0},{2,3},{3,2},{4,5},{5,4},{6,7},{7,6},{8,9},{9,8},{10,11... | collective-permute-start | bytes 1277960 | tf_op jit(solution)/shard_map/ppermute | solution.py:58
  21.8 4.6 %collective-permute-done.12.refs_3_ = f32[416,256]{1,0:T(8,128)S(1)} collective-permute-done((f32[416,256]{1,0:T(8,128)}, f32[416,256]{1,0:T(8,128)S(1)}, u32[]{:S(2)}, u32[]{:S(2)}) %collective-permute-start.12) | collective-permute-done | bytes 426016 | tf_op jit(solution)/shard_map/ppermute | solution.py:54
  26.4 3.5 %collective-permute-start.25 = (f32[416,256]{1,0:T(8,128)S(1)}, f32[416,256]{1,0:T(8,128)S(1)}, u32[]{:S(2)}, u32[]{:S(2)}) collective-permute-start(f32[416,256]{1,0:T(8,128)S(1)} %collective-permute-done.12.refs_3_), channel_id=1, source_target_pairs={{0,1},{1,0},{2,3},{3,2},{4,5},{5,4},{6,7},{7,6},{8,9},{9,8},{10,11... | collective-permute-start | bytes 1277960 | tf_op jit(solution)/shard_map/ppermute | solution.py:58
  29.9 1.0 collective-permute-start.10
  31.0 0.8 copy-done.5
  32.2 0.8 copy-done.7
  33.0 2.7 %collective-permute-start.9 = (f32[416,256]{1,0:T(8,128)S(1)}, f32[416,256]{1,0:T(8,128)S(1)}, u32[]{:S(2)}, u32[]{:S(2)}) collective-permute-start(f32[416,256]{1,0:T(8,128)S(1)} %collective-permute-done.refs_5_), channel_id=1, source_target_pairs={{0,24},{1,7},{2,26},{3,1},{4,28},{5,3},{6,30},{7,5},{8,0},{9,15},{... | collective-permute-start | bytes 1277960 | tf_op jit(solution)/shard_map/ppermute | solution.py:54
  35.7 0.8 copy-done.9
  36.5 0.9 collective-permute-done.10.refs_3_
  37.4 1.2 collective-permute-start.27
  38.5 1.8 %collective-permute-done.1.refs_4_ = f32[416,256]{1,0:T(8,128)} collective-permute-done((f32[416,256]{1,0:T(8,128)S(1)}, f32[416,256]{1,0:T(8,128)}, u32[]{:S(2)}, u32[]{:S(2)}) %collective-permute-start.1) | collective-permute-done | bytes 426016 | tf_op jit(solution)/shard_map/ppermute | solution.py:54
  40.3 2.0 %collective-permute-start.21 = (f32[416,256]{1,0:T(8,128)S(1)}, f32[416,256]{1,0:T(8,128)}, u32[]{:S(2)}, u32[]{:S(2)}) collective-permute-start(f32[416,256]{1,0:T(8,128)S(1)} %collective-permute-done.10.refs_3_), channel_id=1, source_target_pairs={{0,1},{1,0},{2,3},{3,2},{4,5},{5,4},{6,7},{7,6},{8,9},{9,8},{10,11... | collective-permute-start | bytes 1277960 | tf_op jit(solution)/shard_map/ppermute | solution.py:58
  42.3 2.6 %collective-permute-done.20.refs_5_ = f32[416,256]{1,0:T(8,128)} collective-permute-done((f32[416,256]{1,0:T(8,128)S(1)}, f32[416,256]{1,0:T(8,128)}, u32[]{:S(2)}, u32[]{:S(2)}) %collective-permute-start.20) | collective-permute-done | bytes 426016 | tf_op jit(solution)/shard_map/ppermute | solution.py:54
  44.9 2.0 %collective-permute-start.22 = (f32[416,256]{1,0:T(8,128)}, f32[416,256]{1,0:T(8,128)}, u32[]{:S(2)}, u32[]{:S(2)}) collective-permute-start(f32[416,256]{1,0:T(8,128)} %collective-permute-done.1.refs_4_), channel_id=1, source_target_pairs={{0,1},{1,0},{2,3},{3,2},{4,5},{5,4},{6,7},{7,6},{8,9},{9,8},{10,11... | collective-permute-start | bytes 1277960 | tf_op jit(solution)/shard_map/ppermute | solution.py:58
  46.8 0.8 copy-done.3
  47.6 2.0 %shard_map.90 = f32[896,256]{1,0:T(8,128)} custom-call(f32[384,256]{1,0:T(8,128)S(1)} %collective-permute-done.31.rows_ref, s32[1,384]{1,0:T(1,128)S(1)} %collective-permute-done.32.dest_ref), custom_call_target="tpu_custom_call" | custom-call | flops 400000000 | bytes 2000000 | tf_op jit(solution)/shard_map/pallas_call | solution.py:121
  49.6 4.1 %all-to-all-start = ((f32[16,56,256]{2,1,0:T(8,128)}), f32[16,56,256]{2,1,0:T(8,128)S(1)}, u32[]{:S(2)}, u32[]{:S(2)}) async-start(f32[16,56,256]{2,1,0:T(8,128)} %bitcast.7), calls=%async_computation | async-start | bytes 1835008 | tf_op jit(solution)/shard_map/all_to_all | solution.py:445
  53.8 2.6 %collective-permute-start.14 = (f32[416,256]{1,0:T(8,128)}, f32[416,256]{1,0:T(8,128)}, u32[]{:S(2)}, u32[]{:S(2)}) collective-permute-start(f32[416,256]{1,0:T(8,128)} %collective-permute-done.5.refs_5_), channel_id=1, source_target_pairs={{0,24},{1,7},{2,26},{3,1},{4,28},{5,3},{6,30},{7,5},{8,0},{9,15},{... | collective-permute-start | bytes 1277960 | tf_op jit(solution)/shard_map/ppermute | solution.py:54
  56.4 2.7 %collective-permute-start.11 = (f32[416,256]{1,0:T(8,128)S(1)}, f32[416,256]{1,0:T(8,128)}, u32[]{:S(2)}, u32[]{:S(2)}) collective-permute-start(f32[416,256]{1,0:T(8,128)S(1)} %collective-permute-done.10.refs_3_), channel_id=1, source_target_pairs={{0,24},{1,7},{2,26},{3,1},{4,28},{5,3},{6,30},{7,5},{8,0},{9,15},{... | collective-permute-start | bytes 1277960 | tf_op jit(solution)/shard_map/ppermute | solution.py:54
  59.1 1.9 %collective-permute-start.15 = (f32[416,256]{1,0:T(8,128)}, f32[416,256]{1,0:T(8,128)}, u32[]{:S(2)}, u32[]{:S(2)}) collective-permute-start(f32[416,256]{1,0:T(8,128)} %copy-done.3), channel_id=1, source_target_pairs={{0,1},{1,0},{2,3},{3,2},{4,5},{5,4},{6,7},{7,6},{8,9},{9,8},{10,11... | collective-permute-start | bytes 1277960 | tf_op jit(solution)/shard_map/ppermute | solution.py:58
  61.1 10.0 %collective-permute-done.14.refs_7_ = f32[416,256]{1,0:T(8,128)} collective-permute-done((f32[416,256]{1,0:T(8,128)}, f32[416,256]{1,0:T(8,128)}, u32[]{:S(2)}, u32[]{:S(2)}) %collective-permute-start.14) | collective-permute-done | bytes 426016 | tf_op jit(solution)/shard_map/ppermute | solution.py:54
  71.1 1.1 collective-permute-start.6
  72.3 0.7 collective-permute-start.19
  73.0 2.7 %collective-permute-done.11.refs_5_ = f32[416,256]{1,0:T(8,128)} collective-permute-done((f32[416,256]{1,0:T(8,128)S(1)}, f32[416,256]{1,0:T(8,128)}, u32[]{:S(2)}, u32[]{:S(2)}) %collective-permute-start.11) | collective-permute-done | bytes 426016 | tf_op jit(solution)/shard_map/ppermute | solution.py:54
  75.7 2.4 %collective-permute-start.3 = (f32[416,256]{1,0:T(8,128)}, f32[416,256]{1,0:T(8,128)}, u32[]{:S(2)}, u32[]{:S(2)}) collective-permute-start(f32[416,256]{1,0:T(8,128)} %collective-permute-done.2.refs_4_), channel_id=1, source_target_pairs={{0,6},{1,25},{2,0},{3,27},{4,2},{5,29},{6,4},{7,31},{8,14},{9,1},{... | collective-permute-start | bytes 1277960 | tf_op jit(solution)/shard_map/ppermute | solution.py:54
  78.8 0.7 collective-permute-start.16
  79.8 1.0 copy-done.2
  80.8 1.0 copy-done.6
  81.8 4.3 %shard_map.86 = (f32[416,256]{1,0:T(8,128)S(1)}, f32[416,256]{1,0:T(8,128)S(1)}) custom-call(s32[3]{0:T(128)S(1)} %pad_add_fusion.refs_0_.where_ref, s32[1]{0:T(128)} %bitcast.13.refs_1_, f32[416,13312]{1,0:T(8,128)} %bitcast.21, f32[416,256]{1,0:T(8,128)S(1)} %collective-permute-done.28.refs_3_, f32[416,256]{1,0:T(8,128)S(1)} %collective-permute-done.4.refs_4_, ...), custom_call_target="tpu_custom_call" | custom-call | flops 1635778560 | bytes 6389760 | tf_op jit(solution)/shard_map/pallas_call | solution.py:261
  86.2 0.7 copy-done.11
  86.9 0.8 copy-done.14
  87.7 1.5 %shard_map.91 = (f32[416,256]{1,0:T(8,128)S(1)}, f32[416,256]{1,0:T(8,128)S(1)}) custom-call(s32[3]{0:T(128)S(1)} %pad_add_fusion.refs_0_.where_ref, f32[16,56,256]{2,1,0:T(8,128)S(1)} %all-to-all-done.in_ref), custom_call_target="tpu_custom_call" | custom-call | flops 400000000 | bytes 2000000 | tf_op jit(solution)/shard_map/pallas_call | solution.py:153
  89.2 1.0 copy-done.8
  90.2 1.0 copy-done.10
  91.3 1.0 copy-done.12
  92.3 5.3 %shard_map.87.refs_9_ = f32[416,256]{1,0:T(8,128)S(1)} custom-call(s32[3]{0:T(128)S(1)} %pad_add_fusion.refs_0_.where_ref, s32[1]{0:T(128)} %bitcast.14.refs_1_, f32[416,13312]{1,0:T(8,128)} %bitcast.22, f32[416,256]{1,0:T(8,128)S(1)} %collective-permute-done.12.refs_3_, f32[416,256]{1,0:T(8,128)S(1)} %collective-permute-done.24.refs_4_, ...), custom_call_target="tpu_custom_call" | custom-call | flops 1962934272 | bytes 7667712 | tf_op jit(solution)/shard_map/pallas_call | solution.py:261
  98.4 5.6 %shard_map.88.refs_13_ = f32[416,256]{1,0:T(8,128)S(1)} custom-call(s32[3]{0:T(128)S(1)} %pad_add_fusion.refs_0_.where_ref, s32[1]{0:T(128)} %bitcast.15.refs_1_, f32[416,13312]{1,0:T(8,128)} %bitcast.23, f32[416,256]{1,0:T(8,128)S(1)} %collective-permute-done.10.refs_3_, f32[416,256]{1,0:T(8,128)} %collective-permute-done.1.refs_4_, ...), custom_call_target="tpu_custom_call" | custom-call | flops 1962934272 | bytes 7667712 | tf_op jit(solution)/shard_map/pallas_call | solution.py:261
  104.1 8.0 %shard_map.89.refs_7_ = f32[416,256]{1,0:T(8,128)S(1)} custom-call(s32[3]{0:T(128)S(1)} %pad_add_fusion.refs_0_.where_ref, s32[1]{0:T(128)} %bitcast.16.refs_1_, f32[416,13312]{1,0:T(8,128)} %bitcast.24, f32[416,256]{1,0:T(8,128)S(1)} %copy-done.4, f32[416,256]{1,0:T(8,128)} %collective-permute-done.2.refs_4_, f32[416,256]{1,0:T(8,128)} %collective-permute-done.11.refs_5_, ...), custom_call_target="tpu_custom_call" | custom-call | flops 3271557120 | bytes 12779520 | tf_op jit(solution)/shard_map/pallas_call | solution.py:261
  112.2 4.8 %shard_map.92 = (f32[416,256]{1,0:T(8,128)S(1)}, f32[128,256]{1,0:T(8,128)S(1)}) custom-call(s32[3]{0:T(128)S(1)} %pad_add_fusion.refs_0_.where_ref, s32[1]{0:T(128)} %bitcast.17.refs_1_, f32[416,13312]{1,0:T(8,128)} %bitcast.25, f32[416,256]{1,0:T(8,128)} %collective-permute-done.3.refs_3_, f32[416,256]{1,0:T(8,128)} %collective-permute-done.6.refs_4_, ...), custom_call_target="tpu_custom_call" | custom-call | flops 1308622848 | bytes 5111808 | tf_op jit(solution)/shard_map/pallas_call | solution.py:261
  117.5 1.1 collective-permute-done.34.sibling_ref
  118.6 7.2 %shard_map.93 = (f32[416,128]{1,0:T(8,128)}, f32[128,128]{1,0:T(8,128)}) custom-call(s32[3]{0:T(128)S(1)} %pad_add_fusion.refs_0_.where_ref, s32[1]{0:T(128)} %bitcast.18.rank_ref, f32[416,256]{1,0:T(8,128)S(1)} %get-tuple-element.13.sum_ref, f32[416,256]{1,0:T(8,128)S(1)} %copy-done.15, f32[128,256]{1,0:T(8,128)S(1)} %get-tuple-element.15.up_ref, ...), custom_call_target="tpu_custom_call" | custom-call | flops 2000000000 | bytes 2000000 | tf_op jit(solution)/shard_map/pallas_call | solution.py:414
  (66 shorter events, 3.2 us)
Async XLA Ops:
  0.6 116.9 %copy-start = (s32[1,16,128]{2,1,0:T(8,128)S(1)}, s32[1,16,128]{2,1,0:T(8,128)}, u32[]{:S(2)}) copy-start(s32[1,16,128]{2,1,0:T(8,128)} %param.13) | copy-start | bytes 24580
  0.6 19.7 %collective-permute-start.4 = (f32[416,256]{1,0:T(8,128)}, f32[416,256]{1,0:T(8,128)S(1)}, u32[]{:S(2)}, u32[]{:S(2)}) collective-permute-start(f32[416,256]{1,0:T(8,128)} %bitcast.26), channel_id=1, source_target_pairs={{0,2},{1,9},{2,4},{3,11},{4,6},{5,13},{6,0},{7,15},{8,10},{9,17},{... | collective-permute-start | bytes 1277960 | tf_op jit(solution)/shard_map/ppermute | solution.py:54
  3.2 18.5 %collective-permute-start = (f32[416,256]{1,0:T(8,128)}, f32[416,256]{1,0:T(8,128)S(1)}, u32[]{:S(2)}, u32[]{:S(2)}) collective-permute-start(f32[416,256]{1,0:T(8,128)} %bitcast.27), channel_id=1, source_target_pairs={{0,6},{1,25},{2,0},{3,27},{4,2},{5,29},{6,4},{7,31},{8,14},{9,1},{... | collective-permute-start | bytes 1277960 | tf_op jit(solution)/shard_map/ppermute | solution.py:54
  5.4 12.9 %collective-permute-start.31 = (f32[384,256]{1,0:T(8,128)}, f32[384,256]{1,0:T(8,128)S(1)}, u32[]{:S(2)}, u32[]{:S(2)}) collective-permute-start(f32[384,256]{1,0:T(8,128)} %bitcast.31), channel_id=1, source_target_pairs={{0,32},{32,64},{64,96},{96,0},{1,33},{33,65},{65,97},{97,1},{2,34}... | collective-permute-start | bytes 1179656 | tf_op jit(solution)/shard_map/ppermute | solution.py:442
  6.7 11.0 %collective-permute-start.32 = (s32[1,384]{1,0:T(1,128)}, s32[1,384]{1,0:T(1,128)S(1)}, u32[]{:S(2)}, u32[]{:S(2)}) collective-permute-start(s32[1,384]{1,0:T(1,128)} %param.10), channel_id=1, source_target_pairs={{0,32},{32,64},{64,96},{96,0},{1,33},{33,65},{65,97},{97,1},{2,34}... | collective-permute-start | bytes 4616 | tf_op jit(solution)/shard_map/ppermute | solution.py:443
  8.0 13.8 %collective-permute-start.28 = (f32[416,256]{1,0:T(8,128)}, f32[416,256]{1,0:T(8,128)S(1)}, u32[]{:S(2)}, u32[]{:S(2)}) collective-permute-start(f32[416,256]{1,0:T(8,128)} %bitcast.28), channel_id=1, source_target_pairs={{0,1},{1,0},{2,3},{3,2},{4,5},{5,4},{6,7},{7,6},{8,9},{9,8},{10,11... | collective-permute-start | bytes 1277960 | tf_op jit(solution)/shard_map/ppermute | solution.py:58
  17.7 8.7 %collective-permute-start.12 = (f32[416,256]{1,0:T(8,128)}, f32[416,256]{1,0:T(8,128)S(1)}, u32[]{:S(2)}, u32[]{:S(2)}) collective-permute-start(f32[416,256]{1,0:T(8,128)} %bitcast.29), channel_id=1, source_target_pairs={{0,8},{1,3},{2,10},{3,5},{4,12},{5,7},{6,14},{7,1},{8,16},{9,11},{... | collective-permute-start | bytes 1277960 | tf_op jit(solution)/shard_map/ppermute | solution.py:54
  18.2 11.7 %collective-permute-start.24 = (f32[416,256]{1,0:T(8,128)}, f32[416,256]{1,0:T(8,128)S(1)}, u32[]{:S(2)}, u32[]{:S(2)}) collective-permute-start(f32[416,256]{1,0:T(8,128)} %bitcast.30), channel_id=1, source_target_pairs={{0,24},{1,7},{2,26},{3,1},{4,28},{5,3},{6,30},{7,5},{8,0},{9,15},{... | collective-permute-start | bytes 1277960 | tf_op jit(solution)/shard_map/ppermute | solution.py:54
  20.3 9.6 %collective-permute-start.29 = (f32[416,256]{1,0:T(8,128)S(1)}, f32[416,256]{1,0:T(8,128)S(1)}, u32[]{:S(2)}, u32[]{:S(2)}) collective-permute-start(f32[416,256]{1,0:T(8,128)S(1)} %collective-permute-done.4.refs_4_), channel_id=1, source_target_pairs={{0,1},{1,0},{2,3},{3,2},{4,5},{5,4},{6,7},{7,6},{8,9},{9,8},{10,11... | collective-permute-start | bytes 1277960 | tf_op jit(solution)/shard_map/ppermute | solution.py:58
  21.7 9.3 %collective-permute-start.30 = (f32[416,256]{1,0:T(8,128)S(1)}, f32[416,256]{1,0:T(8,128)S(1)}, u32[]{:S(2)}, u32[]{:S(2)}) collective-permute-start(f32[416,256]{1,0:T(8,128)S(1)} %collective-permute-done.refs_5_), channel_id=1, source_target_pairs={{0,1},{1,0},{2,3},{3,2},{4,5},{5,4},{6,7},{7,6},{8,9},{9,8},{10,11... | collective-permute-start | bytes 1277960 | tf_op jit(solution)/shard_map/ppermute | solution.py:58
  21.8 10.4 %collective-permute-start.5 = (f32[416,256]{1,0:T(8,128)S(1)}, f32[416,256]{1,0:T(8,128)}, u32[]{:S(2)}, u32[]{:S(2)}) collective-permute-start(f32[416,256]{1,0:T(8,128)S(1)} %collective-permute-done.4.refs_4_), channel_id=1, source_target_pairs={{0,2},{1,9},{2,4},{3,11},{4,6},{5,13},{6,0},{7,15},{8,10},{9,17},{... | collective-permute-start | bytes 1277960 | tf_op jit(solution)/shard_map/ppermute | solution.py:54
  26.4 5.9 %collective-permute-start.25 = (f32[416,256]{1,0:T(8,128)S(1)}, f32[416,256]{1,0:T(8,128)S(1)}, u32[]{:S(2)}, u32[]{:S(2)}) collective-permute-start(f32[416,256]{1,0:T(8,128)S(1)} %collective-permute-done.12.refs_3_), channel_id=1, source_target_pairs={{0,1},{1,0},{2,3},{3,2},{4,5},{5,4},{6,7},{7,6},{8,9},{9,8},{10,11... | collective-permute-start | bytes 1277960 | tf_op jit(solution)/shard_map/ppermute | solution.py:58
  29.9 5.8 %collective-permute-start.26 = (f32[416,256]{1,0:T(8,128)S(1)}, f32[416,256]{1,0:T(8,128)S(1)}, u32[]{:S(2)}, u32[]{:S(2)}) collective-permute-start(f32[416,256]{1,0:T(8,128)S(1)} %collective-permute-done.24.refs_4_), channel_id=1, source_target_pairs={{0,1},{1,0},{2,3},{3,2},{4,5},{5,4},{6,7},{7,6},{8,9},{9,8},{10,11... | collective-permute-start | bytes 1277960 | tf_op jit(solution)/shard_map/ppermute | solution.py:58
  29.9 19.7 %copy-start.1 = (f32[416,256]{1,0:T(8,128)}, f32[416,256]{1,0:T(8,128)S(1)}, u32[]{:S(2)}) copy-start(f32[416,256]{1,0:T(8,128)S(1)} %collective-permute-done.29.refs_6_) | copy-start | bytes 1277956
  29.9 7.4 %collective-permute-start.10 = (f32[416,256]{1,0:T(8,128)S(1)}, f32[416,256]{1,0:T(8,128)S(1)}, u32[]{:S(2)}, u32[]{:S(2)}) collective-permute-start(f32[416,256]{1,0:T(8,128)S(1)} %collective-permute-done.4.refs_4_), channel_id=1, source_target_pairs={{0,24},{1,7},{2,26},{3,1},{4,28},{5,3},{6,30},{7,5},{8,0},{9,15},{... | collective-permute-start | bytes 1277960 | tf_op jit(solution)/shard_map/ppermute | solution.py:54
  31.7 8.6 %collective-permute-start.1 = (f32[416,256]{1,0:T(8,128)S(1)}, f32[416,256]{1,0:T(8,128)}, u32[]{:S(2)}, u32[]{:S(2)}) collective-permute-start(f32[416,256]{1,0:T(8,128)S(1)} %collective-permute-done.refs_5_), channel_id=1, source_target_pairs={{0,8},{1,3},{2,10},{3,5},{4,12},{5,7},{6,14},{7,1},{8,16},{9,11},{... | collective-permute-start | bytes 1277960 | tf_op jit(solution)/shard_map/ppermute | solution.py:54
  32.2 12.7 %collective-permute-start.20 = (f32[416,256]{1,0:T(8,128)S(1)}, f32[416,256]{1,0:T(8,128)}, u32[]{:S(2)}, u32[]{:S(2)}) collective-permute-start(f32[416,256]{1,0:T(8,128)S(1)} %collective-permute-done.4.refs_4_), channel_id=1, source_target_pairs={{0,8},{1,3},{2,10},{3,5},{4,12},{5,7},{6,14},{7,1},{8,16},{9,11},{... | collective-permute-start | bytes 1277960 | tf_op jit(solution)/shard_map/ppermute | solution.py:54
  32.2 0.8 copy-start.7
  33.0 13.8 %collective-permute-start.9 = (f32[416,256]{1,0:T(8,128)S(1)}, f32[416,256]{1,0:T(8,128)S(1)}, u32[]{:S(2)}, u32[]{:S(2)}) collective-permute-start(f32[416,256]{1,0:T(8,128)S(1)} %collective-permute-done.refs_5_), channel_id=1, source_target_pairs={{0,24},{1,7},{2,26},{3,1},{4,28},{5,3},{6,30},{7,5},{8,0},{9,15},{... | collective-permute-start | bytes 1277960 | tf_op jit(solution)/shard_map/ppermute | solution.py:54
  35.7 0.8 copy-start.9
  36.5 17.3 %collective-permute-start.13 = (f32[416,256]{1,0:T(8,128)S(1)}, f32[416,256]{1,0:T(8,128)}, u32[]{:S(2)}, u32[]{:S(2)}) collective-permute-start(f32[416,256]{1,0:T(8,128)S(1)} %collective-permute-done.12.refs_3_), channel_id=1, source_target_pairs={{0,8},{1,3},{2,10},{3,5},{4,12},{5,7},{6,14},{7,1},{8,16},{9,11},{... | collective-permute-start | bytes 1277960 | tf_op jit(solution)/shard_map/ppermute | solution.py:54
  37.4 19.1 %collective-permute-start.27 = (f32[416,256]{1,0:T(8,128)}, f32[416,256]{1,0:T(8,128)}, u32[]{:S(2)}, u32[]{:S(2)}) collective-permute-start(f32[416,256]{1,0:T(8,128)} %collective-permute-done.5.refs_5_), channel_id=1, source_target_pairs={{0,1},{1,0},{2,3},{3,2},{4,5},{5,4},{6,7},{7,6},{8,9},{9,8},{10,11... | collective-permute-start | bytes 1277960 | tf_op jit(solution)/shard_map/ppermute | solution.py:58
  40.3 16.1 %collective-permute-start.21 = (f32[416,256]{1,0:T(8,128)S(1)}, f32[416,256]{1,0:T(8,128)}, u32[]{:S(2)}, u32[]{:S(2)}) collective-permute-start(f32[416,256]{1,0:T(8,128)S(1)} %collective-permute-done.10.refs_3_), channel_id=1, source_target_pairs={{0,1},{1,0},{2,3},{3,2},{4,5},{5,4},{6,7},{7,6},{8,9},{9,8},{10,11... | collective-permute-start | bytes 1277960 | tf_op jit(solution)/shard_map/ppermute | solution.py:58
  44.9 14.2 %collective-permute-start.22 = (f32[416,256]{1,0:T(8,128)}, f32[416,256]{1,0:T(8,128)}, u32[]{:S(2)}, u32[]{:S(2)}) collective-permute-start(f32[416,256]{1,0:T(8,128)} %collective-permute-done.1.refs_4_), channel_id=1, source_target_pairs={{0,1},{1,0},{2,3},{3,2},{4,5},{5,4},{6,7},{7,6},{8,9},{9,8},{10,11... | collective-permute-start | bytes 1277960 | tf_op jit(solution)/shard_map/ppermute | solution.py:58
  47.6 13.4 %collective-permute-start.23 = (f32[416,256]{1,0:T(8,128)}, f32[416,256]{1,0:T(8,128)}, u32[]{:S(2)}, u32[]{:S(2)}) collective-permute-start(f32[416,256]{1,0:T(8,128)} %collective-permute-done.20.refs_5_), channel_id=1, source_target_pairs={{0,1},{1,0},{2,3},{3,2},{4,5},{5,4},{6,7},{7,6},{8,9},{9,8},{10,11... | collective-permute-start | bytes 1277960 | tf_op jit(solution)/shard_map/ppermute | solution.py:58
  49.6 38.1 %all-to-all-start = ((f32[16,56,256]{2,1,0:T(8,128)}), f32[16,56,256]{2,1,0:T(8,128)S(1)}, u32[]{:S(2)}, u32[]{:S(2)}) async-start(f32[16,56,256]{2,1,0:T(8,128)} %bitcast.7), calls=%async_computation | async-start | bytes 1835008 | tf_op jit(solution)/shard_map/all_to_all | solution.py:445
  53.8 17.3 %collective-permute-start.14 = (f32[416,256]{1,0:T(8,128)}, f32[416,256]{1,0:T(8,128)}, u32[]{:S(2)}, u32[]{:S(2)}) collective-permute-start(f32[416,256]{1,0:T(8,128)} %collective-permute-done.5.refs_5_), channel_id=1, source_target_pairs={{0,24},{1,7},{2,26},{3,1},{4,28},{5,3},{6,30},{7,5},{8,0},{9,15},{... | collective-permute-start | bytes 1277960 | tf_op jit(solution)/shard_map/ppermute | solution.py:54
  56.4 15.9 %collective-permute-start.2 = (f32[416,256]{1,0:T(8,128)}, f32[416,256]{1,0:T(8,128)}, u32[]{:S(2)}, u32[]{:S(2)}) collective-permute-start(f32[416,256]{1,0:T(8,128)} %collective-permute-done.1.refs_4_), channel_id=1, source_target_pairs={{0,8},{1,3},{2,10},{3,5},{4,12},{5,7},{6,14},{7,1},{8,16},{9,11},{... | collective-permute-start | bytes 1277960 | tf_op jit(solution)/shard_map/ppermute | solution.py:54
  56.4 19.2 %collective-permute-start.11 = (f32[416,256]{1,0:T(8,128)S(1)}, f32[416,256]{1,0:T(8,128)}, u32[]{:S(2)}, u32[]{:S(2)}) collective-permute-start(f32[416,256]{1,0:T(8,128)S(1)} %collective-permute-done.10.refs_3_), channel_id=1, source_target_pairs={{0,24},{1,7},{2,26},{3,1},{4,28},{5,3},{6,30},{7,5},{8,0},{9,15},{... | collective-permute-start | bytes 1277960 | tf_op jit(solution)/shard_map/ppermute | solution.py:54
  59.1 19.7 %collective-permute-start.15 = (f32[416,256]{1,0:T(8,128)}, f32[416,256]{1,0:T(8,128)}, u32[]{:S(2)}, u32[]{:S(2)}) collective-permute-start(f32[416,256]{1,0:T(8,128)} %copy-done.3), channel_id=1, source_target_pairs={{0,1},{1,0},{2,3},{3,2},{4,5},{5,4},{6,7},{7,6},{8,9},{9,8},{10,11... | collective-permute-start | bytes 1277960 | tf_op jit(solution)/shard_map/ppermute | solution.py:58
  61.0 18.5 %collective-permute-start.18 = (f32[416,256]{1,0:T(8,128)}, f32[416,256]{1,0:T(8,128)}, u32[]{:S(2)}, u32[]{:S(2)}) collective-permute-start(f32[416,256]{1,0:T(8,128)} %collective-permute-done.13.refs_6_), channel_id=1, source_target_pairs={{0,1},{1,0},{2,3},{3,2},{4,5},{5,4},{6,7},{7,6},{8,9},{9,8},{10,11... | collective-permute-start | bytes 1277960 | tf_op jit(solution)/shard_map/ppermute | solution.py:58
  71.1 26.5 %collective-permute-start.6 = (f32[416,256]{1,0:T(8,128)}, f32[416,256]{1,0:T(8,128)}, u32[]{:S(2)}, u32[]{:S(2)}) collective-permute-start(f32[416,256]{1,0:T(8,128)} %collective-permute-done.5.refs_5_), channel_id=1, source_target_pairs={{0,8},{1,3},{2,10},{3,5},{4,12},{5,7},{6,14},{7,1},{8,16},{9,11},{... | collective-permute-start | bytes 1277960 | tf_op jit(solution)/shard_map/ppermute | solution.py:54
  72.3 25.6 %collective-permute-start.19 = (f32[416,256]{1,0:T(8,128)}, f32[416,256]{1,0:T(8,128)}, u32[]{:S(2)}, u32[]{:S(2)}) collective-permute-start(f32[416,256]{1,0:T(8,128)} %collective-permute-done.14.refs_7_), channel_id=1, source_target_pairs={{0,1},{1,0},{2,3},{3,2},{4,5},{5,4},{6,7},{7,6},{8,9},{9,8},{10,11... | collective-permute-start | bytes 1277960 | tf_op jit(solution)/shard_map/ppermute | solution.py:58
  75.7 22.5 %collective-permute-start.3 = (f32[416,256]{1,0:T(8,128)}, f32[416,256]{1,0:T(8,128)}, u32[]{:S(2)}, u32[]{:S(2)}) collective-permute-start(f32[416,256]{1,0:T(8,128)} %collective-permute-done.2.refs_4_), channel_id=1, source_target_pairs={{0,6},{1,25},{2,0},{3,27},{4,2},{5,29},{6,4},{7,31},{8,14},{9,1},{... | collective-permute-start | bytes 1277960 | tf_op jit(solution)/shard_map/ppermute | solution.py:54
  78.8 25.2 %collective-permute-start.16 = (f32[416,256]{1,0:T(8,128)}, f32[416,256]{1,0:T(8,128)}, u32[]{:S(2)}, u32[]{:S(2)}) collective-permute-start(f32[416,256]{1,0:T(8,128)} %collective-permute-done.2.refs_4_), channel_id=1, source_target_pairs={{0,1},{1,0},{2,3},{3,2},{4,5},{5,4},{6,7},{7,6},{8,9},{9,8},{10,11... | collective-permute-start | bytes 1277960 | tf_op jit(solution)/shard_map/ppermute | solution.py:58
  79.5 24.5 %collective-permute-start.17 = (f32[416,256]{1,0:T(8,128)}, f32[416,256]{1,0:T(8,128)}, u32[]{:S(2)}, u32[]{:S(2)}) collective-permute-start(f32[416,256]{1,0:T(8,128)} %collective-permute-done.11.refs_5_), channel_id=1, source_target_pairs={{0,1},{1,0},{2,3},{3,2},{4,5},{5,4},{6,7},{7,6},{8,9},{9,8},{10,11... | collective-permute-start | bytes 1277960 | tf_op jit(solution)/shard_map/ppermute | solution.py:58
  79.8 1.0 copy-start.2
  80.8 1.0 copy-start.6
  89.2 1.0 copy-start.8
  90.2 1.0 copy-start.10
  91.3 1.0 copy-start.12
  92.3 11.8 %copy-start.4 = (f32[416,256]{1,0:T(8,128)S(1)}, f32[416,256]{1,0:T(8,128)}, u32[]{:S(2)}) copy-start(f32[416,256]{1,0:T(8,128)} %copy-done.3) | copy-start | bytes 1277956
  97.6 14.5 %collective-permute-start.33 = (f32[416,256]{1,0:T(8,128)S(1)}, f32[416,256]{1,0:T(8,128)S(1)}, u32[]{:S(2)}, u32[]{:S(2)}) collective-permute-start(f32[416,256]{1,0:T(8,128)S(1)} %get-tuple-element.12), channel_id=1, source_target_pairs={{0,1},{1,0},{2,3},{3,2},{4,5},{5,4},{6,7},{7,6},{8,9},{9,8},{10,11... | collective-permute-start | bytes 1277960 | tf_op jit(solution)/shard_map/ppermute | solution.py:58
  97.9 14.2 %collective-permute-start.8 = (f32[416,256]{1,0:T(8,128)}, f32[416,256]{1,0:T(8,128)S(1)}, u32[]{:S(2)}, u32[]{:S(2)}) collective-permute-start(f32[416,256]{1,0:T(8,128)} %collective-permute-done.6.refs_4_), channel_id=1, source_target_pairs={{0,1},{1,0},{2,3},{3,2},{4,5},{5,4},{6,7},{7,6},{8,9},{9,8},{10,11... | collective-permute-start | bytes 1277960 | tf_op jit(solution)/shard_map/ppermute | solution.py:58
  98.2 13.9 %collective-permute-start.7 = (f32[416,256]{1,0:T(8,128)}, f32[416,256]{1,0:T(8,128)S(1)}, u32[]{:S(2)}, u32[]{:S(2)}) collective-permute-start(f32[416,256]{1,0:T(8,128)} %collective-permute-done.3.refs_3_), channel_id=1, source_target_pairs={{0,1},{1,0},{2,3},{3,2},{4,5},{5,4},{6,7},{7,6},{8,9},{9,8},{10,11... | collective-permute-start | bytes 1277960 | tf_op jit(solution)/shard_map/ppermute | solution.py:58
  98.4 13.7 %copy-start.13 = (s32[1,1,128]{2,1,0:T(1,128)S(1)}, s32[1,1,128]{2,1,0:T(1,128)}, u32[]{:S(2)}) copy-start(s32[1,1,128]{2,1,0:T(1,128)} %param.11) | copy-start | bytes 1540
  104.1 14.5 %copy-start.15 = (f32[416,256]{1,0:T(8,128)S(1)}, f32[416,256]{1,0:T(8,128)}, u32[]{:S(2)}) copy-start(f32[416,256]{1,0:T(8,128)} %copy-done.14) | copy-start | bytes 1277956
  116.9 1.6 %collective-permute-start.34 = (f32[128,256]{1,0:T(8,128)S(1)}, f32[128,256]{1,0:T(8,128)S(1)}, u32[]{:S(2)}, u32[]{:S(2)}) collective-permute-start(f32[128,256]{1,0:T(8,128)S(1)} %get-tuple-element.15.up_ref), channel_id=1, source_target_pairs={{0,1},{1,0},{2,3},{3,2},{4,5},{5,4},{6,7},{7,6},{8,9},{9,8},{10,11... | collective-permute-start | bytes 393224 | tf_op jit(solution)/shard_map/ppermute | solution.py:58
  (4 other events, 3.0 us)
